TPU v7x, 32 devices: a whole 2x2x4 slice. The times are simulated.
32 devices in a mesh: tensor: 2 (over y), context: 16 (over z, x, core).
Axes of the slice: x: 2, y: 2, z: 4, core: 2. Of those that a mesh axis runs over, the one named last changes fastest.
Arguments:
- hidden_in: bfloat16 [8192, 4096], P('context', 'tensor'), may hold values from -6 to 6
- norm_gain: bfloat16 [4096], replicated, may hold values from 0.099609375 to 1.8984375
- w_query: bfloat16 [4096, 4096], P('context', 'tensor'), may hold values from -0.09375 to 0.09375
- w_key: bfloat16 [4096, 1024], P('context', 'tensor'), may hold values from -0.09375 to 0.09375
- w_value: bfloat16 [4096, 1024], P('context', 'tensor'), may hold values from -0.09375 to 0.09375
- kv_cache: bfloat16 [16384, 2, 1024], P('context', None, 'tensor'), may hold values from -68 to 68
- selected: int32 [16, 3], replicated, may hold values from 0 to 127, as said below
Outputs:
- attended: bfloat16 [8192, 4096], P('context', 'tensor')
Inputs may be any that keep to these rules, and one draw needn't show every extreme that they name: `selected`: each row names 3 cache blocks held by 3 different devices of context (block c is held by device c // 8). The blocks held by one device are named at most 6 times over all rows together, and those of one device exactly 6 times.
All inputs are finite; a program needn't handle non-finite values.
Results may differ from a plain program's by a relative error of at most 0.011.
The roundings to bfloat16 on the way count: a program that leaves them out, or rounds other values in their place, can miss the bound.
Values may be sent and summed in bfloat16 or wider, within the bound.
A program may use at most 128 MiB of HBM per device.

v0:
```python
import math

import jax
import jax.numpy as jnp
from jax import lax
from jax.sharding import PartitionSpec as P

HEAD_DIM = 128
C_BLOCK = 128
PICKS = 3
MOST_REQ = 6
BLOCKS_DEV = 8


def on_device(hidden_in, norm_gain, w_query, w_key, w_value, kv_cache, selected):
    gathered = lax.all_gather(hidden_in, "tensor", axis=1, tiled=True)
    floats = gathered.astype(jnp.float32)
    inverse_rms = lax.rsqrt(jnp.mean(floats * floats, axis=1, keepdims=True) + 1e-05)
    normed = (floats * inverse_rms * norm_gain.astype(jnp.float32)).astype(jnp.bfloat16)
    row_count = normed.shape[0]
    query_cols = w_query.shape[1]
    key_cols = w_key.shape[1]
    stacked = jnp.concatenate([w_query, w_key, w_value], axis=1)
    projected = jnp.dot(
        normed,
        lax.all_gather(stacked, "context", axis=0, tiled=True),
        preferred_element_type=jnp.float32,
    )
    query = projected[:, :query_cols].astype(jnp.bfloat16)
    fresh_key = projected[:, query_cols : query_cols + key_cols].astype(jnp.bfloat16)
    fresh_value = projected[:, query_cols + key_cols :].astype(jnp.bfloat16)
    local_heads = kv_cache.shape[2] // HEAD_DIM
    devices = lax.axis_size("context")
    myself = lax.axis_index("context")
    owners = selected // BLOCKS_DEV
    offsets = selected % BLOCKS_DEV
    blocks = kv_cache.reshape(BLOCKS_DEV, C_BLOCK, 2, local_heads, HEAD_DIM)
    listings = devices * PICKS
    piece_rows = C_BLOCK // devices
    flat_owner = owners.reshape(listings)
    flat_offset = offsets.reshape(listings)
    serial = jnp.arange(listings, dtype=jnp.int32)
    earlier = (flat_owner[:, None] == flat_owner[None, :]) & (serial[:, None] > serial[None, :])
    ranks = jnp.sum(earlier.astype(jnp.int32), axis=1)
    slots = jnp.arange(MOST_REQ, dtype=jnp.int32)
    hits = (flat_owner[None, :] == myself) & (ranks[None, :] == slots[:, None])
    filled = jnp.any(hits, axis=1)
    picked = jnp.sum(jnp.where(hits, flat_offset[None, :], 0), axis=1)
    outbox = jnp.where(
        filled[:, None, None, None, None],
        jnp.take(blocks, picked, axis=0),
        jnp.zeros((), jnp.bfloat16),
    )
    outbox = outbox.reshape(MOST_REQ, devices, piece_rows, 2, local_heads, HEAD_DIM)
    spread = lax.all_to_all(outbox, "context", split_axis=1, concat_axis=1, tiled=True)
    relayed = spread.reshape(MOST_REQ * devices, piece_rows, 2, local_heads, HEAD_DIM)
    forward = jnp.take(relayed, ranks * devices + flat_owner, axis=0)
    forward = forward.reshape(devices, PICKS, piece_rows, 2, local_heads, HEAD_DIM)
    collected = lax.all_to_all(forward, "context", split_axis=0, concat_axis=2, tiled=True)
    fetched = collected[0]
    cached = fetched.shape[0] * fetched.shape[1]
    keys_all = jnp.concatenate(
        [
            fetched[:, :, 0].reshape(cached, local_heads, HEAD_DIM),
            fresh_key.reshape(row_count, local_heads, HEAD_DIM),
        ],
        axis=0,
    )
    values_all = jnp.concatenate(
        [
            fetched[:, :, 1].reshape(cached, local_heads, HEAD_DIM),
            fresh_value.reshape(row_count, local_heads, HEAD_DIM),
        ],
        axis=0,
    )
    groups = query.shape[1] // (HEAD_DIM * local_heads)
    grouped = query.reshape(row_count, local_heads, groups, HEAD_DIM)
    score_scale = 1.0 / math.sqrt(HEAD_DIM)
    scores = (
        jnp.einsum("qhgd,khd->hgqk", grouped, keys_all, preferred_element_type=jnp.float32)
        * score_scale
    )
    row_index = jnp.arange(row_count, dtype=jnp.int32)[:, None]
    col_index = jnp.arange(cached + row_count, dtype=jnp.int32)[None, :]
    visible = (col_index < cached) | (col_index - cached <= row_index)
    scores = jnp.where(visible[None, None], scores, -jnp.inf)
    probs = jax.nn.softmax(scores, axis=-1).astype(jnp.bfloat16)
    mixed = jnp.einsum("hgqk,khd->qhgd", probs, values_all, preferred_element_type=jnp.float32)
    return mixed.astype(jnp.bfloat16).reshape(row_count, local_heads * groups * HEAD_DIM)


def solution(mesh):
    return jax.shard_map(
        on_device,
        mesh=mesh,
        in_specs=(
            P("context", "tensor"),
            P(),
            P("context", "tensor"),
            P("context", "tensor"),
            P("context", "tensor"),
            P("context", None, "tensor"),
            P(),
        ),
        out_specs=P("context", "tensor"),
        check_vma=False,
    )
```

profile of v0, /device:TPU:13, one launch (start us, length us, event | category | flops | bytes accessed | tf_op | source)
XLA Modules:
  0.0 270.4 jit_solution(2681840620839282887)
XLA Ops:
  6.5 0.0 all-gather.3.cloned.1.call-start
  6.5 0.7 all-gather.3.cloned.1.call-update
  7.3 0.0 all-gather.5.cloned.1.call-start
  7.3 2.7 %pad_maximum_fusion = bf16[256,3072]{1,0:T(8,128)(2,1)} fusion(bf16[256,512]{1,0:T(8,128)(2,1)} %param.11, bf16[256,512]{1,0:T(8,128)(2,1)} %param.10, bf16[256,2048]{1,0:T(8,128)(2,1)} %param.9), kind=kLoop, calls=%fused_computation.26 | loop fusion | flops 4718592 | bytes 3145728 | tf_op jit(solution)/shard_map/concatenate | solution.py:23
  10.0 0.0 all-gather.5.cloned.1.call-update
  10.1 0.0 copy-start.3
  10.1 3.2 %reshape.176 = bf16[8,128,2,4,128]{4,3,2,1,0:T(4,128)(2,1)S(1)} reshape(bf16[1024,2,512]{2,1,0:T(2,128)(2,1)} %param.12) | data formatting | bytes 4194304 | tf_op jit(solution)/shard_map/reshape | solution.py:37
  13.2 1.9 copy.108
  15.1 0.0 copy-done.3
  15.1 0.1 copy.103
  15.2 0.1 broadcast_in_dim.72
  15.3 0.1 eq.41
  15.4 0.2 convert_reduce_fusion
  15.6 0.1 select_reduce_fusion
  15.7 2.7 %gather_fusion = bf16[6,128,2,4,128]{4,1,3,2,0:T(8,128)(2,1)S(1)} fusion(bf16[8,128,2,4,128]{4,1,3,2,0:T(8,128)(2,1)} %copy.108, s32[1024]{0:T(1024)S(1)} %pad_clamp_fusion.1), kind=kCustom, calls=%fused_computation | custom fusion | bytes 3145752 | tf_op jit(solution)/shard_map/jit(_take)/gather | solution.py:51
  18.5 0.1 fusion.42
  18.6 0.2 fusion.23
  18.8 1.6 copy.109
  20.4 6.6 %all-to-all-start = ((bf16[6,16,8,2,4,128]{5,2,4,3,0,1:T(8,128)(2,1)}), bf16[6,16,8,2,4,128]{5,2,4,3,0,1:T(8,128)(2,1)S(1)}, u32[]{:S(2)}, u32[]{:S(2)}) async-start(bf16[6,16,8,2,4,128]{5,2,4,3,0,1:T(8,128)(2,1)} %copy.109), calls=%async_computation | async-start | bytes 3145728 | tf_op jit(solution)/shard_map/all_to_all | solution.py:55
  27.0 0.1 reshape.153
  27.1 0.1 mul.52
  27.2 35.2 %all-to-all-done = bf16[6,16,8,2,4,128]{5,2,4,3,0,1:T(8,128)(2,1)S(1)} async-done(((bf16[6,16,8,2,4,128]{5,2,4,3,0,1:T(8,128)(2,1)}), bf16[6,16,8,2,4,128]{5,2,4,3,0,1:T(8,128)(2,1)S(1)}, u32[]{:S(2)}, u32[]{:S(2)}) %all-to-all-start) | async-done | bytes 1572896 | tf_op jit(solution)/shard_map/all_to_all | solution.py:55
  62.5 0.4 copy.110
  62.9 0.0 copy-start.2
  62.9 0.7 gather_fusion.1
  63.6 1.0 broadcast_select_fusion
  64.6 5.6 %all-to-all-start.1 = ((bf16[16,3,8,2,4,128]{5,2,4,3,1,0:T(8,128)(2,1)}), bf16[16,3,8,2,4,128]{5,2,4,3,1,0:T(8,128)(2,1)S(1)}, u32[]{:S(2)}, u32[]{:S(2)}) async-start(bf16[16,3,8,2,4,128]{5,2,4,3,1,0:T(8,128)(2,1)} %broadcast_select_fusion), calls=%async_computation.1 | async-start | bytes 1572864 | tf_op jit(solution)/shard_map/all_to_all | solution.py:59
  70.2 0.0 copy-done.2
  70.3 1.2 fusion.22
  71.4 0.0 all-gather.3.cloned.1.call-done
  71.4 3.1 %fusion.8 = f32[512]{0:T(512)S(1)} fusion(bf16[512,4096]{1,0:T(8,128)(2,1)} %all-gather.3.cloned.1.call-done), kind=kLoop, calls=%fused_computation.14 | loop fusion | flops 6290944 | bytes 4196352 | tf_op jit(solution)/shard_map/reduce_sum | solution.py:18
  74.5 21.7 %all-to-all-done.1 = bf16[16,3,8,2,4,128]{5,2,4,3,1,0:T(8,128)(2,1)S(1)} async-done(((bf16[16,3,8,2,4,128]{5,2,4,3,1,0:T(8,128)(2,1)}), bf16[16,3,8,2,4,128]{5,2,4,3,1,0:T(8,128)(2,1)S(1)}, u32[]{:S(2)}, u32[]{:S(2)}) %all-to-all-start.1) | async-done | bytes 786464 | tf_op jit(solution)/shard_map/all_to_all | solution.py:59
  96.2 0.2 copy_bitcast_fusion
  96.4 0.1 fusion.60
  96.6 0.9 copy.113
  97.5 112.4 %all-gather.5.cloned.1.call-done = bf16[4096,3072]{1,0:T(8,128)(2,1)} async-done(((bf16[256,3072]{1,0:T(8,128)(2,1)}), bf16[4096,3072]{1,0:T(8,128)(2,1)}) %all-gather.5.cloned.1.call-update) | async-done | bytes 25165840 | tf_op jit(solution)/shard_map/all_gather | solution.py:26
  210.0 18.2 %convolution_convert_fusion = bf16[512,3072]{1,0:T(8,128)(2,1)S(1)} fusion(bf16[4096,3072]{1,0:T(8,128)(2,1)} %all-gather.5.cloned.1.call-done, bf16[512,4096]{1,0:T(8,128)(2,1)} %all-gather.3.cloned.1.call-done, f32[4096]{0:T(1024)S(1)} %convert_element_type.26, f32[512]{0:T(512)S(1)} %add_rsqrt_fusion), kind=kOutput, calls=%fused_computation.17 | convolution fusion | flops 12894863360 | bytes 32524288 | tf_op jit(solution)/shard_map/dot_general | solution.py:24
  228.2 0.2 slice.31
  228.4 0.1 fusion.59
  228.5 2.7 reshape.156
  231.2 0.9 copy.149
  232.1 0.2 copy.125
  232.3 0.0 copy-start
  232.3 0.0 copy-start.1
  232.3 12.0 %fusion.61 = f32[4,4,512]{2,1,0:T(4,128)} fusion(pred[512,896]{0,1:T(8,128)(4,1)} %fusion.22, bf16[512,4,4,128]{3,2,1,0:T(4,128)(2,1)} %reshape.156, bf16[512,4,128]{2,0,1:T(8,128)(2,1)} %bitcast.79, bf16[384,4,128]{2,0,1:T(8,128)(2,1)S(1)} %bitcast.82), kind=kOutput, calls=%fused_computation.77 | convolution fusion | flops 1910244224 | bytes 3506176 | tf_op jit(solution)/shard_map/sub | solution.py:87
  244.3 0.0 copy-done
  244.3 0.0 copy-done.1
  244.3 15.4 %fusion.14 = bf16[4,128,4,512]{3,1,2,0:T(8,128)(2,1)} fusion(f32[4,4,512]{2,1,0:T(4,128)} %fusion.61, bf16[512,4,128]{0,2,1:T(8,128)(2,1)S(1)} %bitcast.81, bf16[384,4,128]{0,2,1:T(8,128)(2,1)} %copy.113, pred[512,896]{0,1:T(8,128)(4,1)} %fusion.22, bf16[512,4,4,128]{3,2,1,0:T(4,128)(2,1)S(1)} %copy-done, bf16[512,4,128]{2,0,1:T(8,128)(2,1)S(1)} %bitcast.80, ...), kind=kOutput, calls=%fused_computation.20 | convolution fusion | flops 3799524352 | bytes 6520832 | tf_op jit(solution)/shard_map/hgqk,khd->qhgd/dot_general | solution.py:88
  259.7 3.9 %copy.119 = bf16[512,2048]{1,0:T(8,128)(2,1)} copy(bf16[512,2048]{0,1:T(8,128)(2,1)} %bitcast.77) | data formatting | bytes 4194304 | tf_op jit(solution)/shard_map/reshape | solution.py:89
  (15 shorter events, 0.2 us)
Async XLA Ops:
  6.5 64.9 %all-gather.3.cloned.1.call-start = ((), (), s32[]{:S(2)}) async-start(), calls=%async_computation.2 | async-start | bytes 6291456 | tf_op jit(solution)/shard_map/all_gather | solution.py:16
  7.3 202.7 %all-gather.5.cloned.1.call-start = ((), (), s32[]{:S(2)}) async-start(), calls=%async_computation.3 | async-start | bytes 26738688 | tf_op jit(solution)/shard_map/all_gather | solution.py:26
  10.1 5.1 %copy-start.3 = (s32[16,3]{0,1:T(4,128)S(1)}, s32[16,3]{0,1:T(4,128)}, u32[]{:S(2)}) copy-start(s32[16,3]{0,1:T(4,128)} %param.13) | copy-start | bytes 580
  20.4 42.0 %all-to-all-start = ((bf16[6,16,8,2,4,128]{5,2,4,3,0,1:T(8,128)(2,1)}), bf16[6,16,8,2,4,128]{5,2,4,3,0,1:T(8,128)(2,1)S(1)}, u32[]{:S(2)}, u32[]{:S(2)}) async-start(bf16[6,16,8,2,4,128]{5,2,4,3,0,1:T(8,128)(2,1)} %copy.109), calls=%async_computation | async-start | bytes 3145728 | tf_op jit(solution)/shard_map/all_to_all | solution.py:55
  62.9 7.4 %copy-start.2 = (bf16[4096]{0:T(1024)(128)(2,1)S(1)}, bf16[4096]{0:T(1024)(128)(2,1)}, u32[]{:S(2)}) copy-start(bf16[4096]{0:T(1024)(128)(2,1)} %param.8) | copy-start | bytes 24580
  64.6 31.6 %all-to-all-start.1 = ((bf16[16,3,8,2,4,128]{5,2,4,3,1,0:T(8,128)(2,1)}), bf16[16,3,8,2,4,128]{5,2,4,3,1,0:T(8,128)(2,1)S(1)}, u32[]{:S(2)}, u32[]{:S(2)}) async-start(bf16[16,3,8,2,4,128]{5,2,4,3,1,0:T(8,128)(2,1)} %broadcast_select_fusion), calls=%async_computation.1 | async-start | bytes 1572864 | tf_op jit(solution)/shard_map/all_to_all | solution.py:59
  232.3 12.0 %copy-start = (bf16[512,4,4,128]{3,2,1,0:T(4,128)(2,1)S(1)}, bf16[512,4,4,128]{3,2,1,0:T(4,128)(2,1)}, u32[]{:S(2)}) copy-start(bf16[512,4,4,128]{3,2,1,0:T(4,128)(2,1)} %reshape.156) | copy-start | bytes 6291460
  232.3 12.0 %copy-start.1 = (bf16[64,4,8,128]{3,2,0,1:T(8,128)(2,1)S(1)}, bf16[64,4,8,128]{3,2,0,1:T(8,128)(2,1)}, u32[]{:S(2)}) copy-start(bf16[64,4,8,128]{3,2,0,1:T(8,128)(2,1)} %copy.149) | copy-start | bytes 1572868
Sparse Core Ops, SparseCore 0:
  8.9 56.9 all-gather.2
  67.5 142.4 all-gather.4
where the time goes:
time: 271 us; the launch traced here: 270 us
  waiting for transfers between devices  170 us (63%)
  matrix products  45.6 us (17%)
  local copies, waits for them, and re-layouts  20.1 us (7%)
  between operations  13.6 us (5%)
  starting transfers between devices  12.3 us (5%)
  other arithmetic  8.76 us (3%)
    all_gather x1, waiting for transfers between devices, on_device(): lax.all_gather(stacked, 'context', axis=0, tiled=True)  112 us
    all_to_all x1, waiting for transfers between devices, on_device(): lax.all_to_all(outbox, 'context', split_axis=1, concat_axis=1, tiled=True)  35.2 us
    all_to_all x1, waiting for transfers between devices, on_device(): lax.all_to_all(forward, 'context', split_axis=0, concat_axis=2, tiled=True)  21.7 us
    dot_general x1, matrix products, on_device(): jnp.dot(normed, lax.all_gather(stacked, 'context', axis=0, tiled=True), p...  18.2 us
    dot_general x1, matrix products, on_device(): jnp.einsum('hgqk,khd->qhgd', probs, values_all, preferred_element_type=jn...  15.4 us
    sub x1, matrix products, on_device(): probs = jax.nn.softmax(scores, axis=-1).astype(jnp.bfloat16)  12 us
    all_to_all x1, starting transfers between devices, on_device(): lax.all_to_all(outbox, 'context', split_axis=1, concat_axis=1, tiled=True)  6.58 us
    all_to_all x1, starting transfers between devices, on_device(): lax.all_to_all(forward, 'context', split_axis=0, concat_axis=2, tiled=True)  5.64 us
  transfers between devices with their start and end apart: 4, of which 3 were waited for; matrix products, arithmetic and copies ran while one was open for 8% of the time, Pallas kernels for 0%

commit v1 on v0

v1 whole, which is shorter than its diff:
```python
import math

import jax
import jax.numpy as jnp
from jax import lax
from jax.experimental import pallas as pl
from jax.experimental.pallas import tpu as pltpu
from jax.sharding import PartitionSpec as P

HEAD_DIM = 128
C_BLOCK = 128
PICKS = 3
MOST_REQ = 6
BLOCKS_DEV = 8
ROW_TILE = 256


def attend_kernel(q_ref, k_ref, v_ref, ck_ref, cv_ref, *rest):
    o_ref = rest[-1]
    rows = q_ref.shape[0]
    scale = 1.0 / math.sqrt(HEAD_DIM)
    dims = (((1,), (1,)), ((), ()))
    for start in range(0, rows, ROW_TILE):
        stop = start + ROW_TILE
        query = q_ref[start:stop, :]
        cached = lax.dot_general(query, ck_ref[...], dims, preferred_element_type=jnp.float32) * scale
        fresh = lax.dot_general(query, k_ref[:stop, :], dims, preferred_element_type=jnp.float32) * scale
        row = lax.broadcasted_iota(jnp.int32, fresh.shape, 0) + start
        col = lax.broadcasted_iota(jnp.int32, fresh.shape, 1)
        fresh = jnp.where(col <= row, fresh, -jnp.inf)
        top = jnp.maximum(jnp.max(cached, axis=1, keepdims=True), jnp.max(fresh, axis=1, keepdims=True))
        cached = jnp.exp(cached - top)
        fresh = jnp.exp(fresh - top)
        total = jnp.sum(cached, axis=1, keepdims=True) + jnp.sum(fresh, axis=1, keepdims=True)
        inverse = 1.0 / total
        mixed = jnp.dot(
            (cached * inverse).astype(jnp.bfloat16), cv_ref[...], preferred_element_type=jnp.float32
        )
        mixed += jnp.dot(
            (fresh * inverse).astype(jnp.bfloat16), v_ref[:stop, :], preferred_element_type=jnp.float32
        )
        o_ref[start:stop, :] = mixed.astype(o_ref.dtype)


def attend(projected, cached_key, cached_value, earlier, group, groups, local_heads):
    rows = projected.shape[0]
    cached = cached_key.shape[0]
    column = lambda place: pl.BlockSpec((rows, HEAD_DIM), lambda h: (0, place))
    operands = [projected, projected, projected, cached_key, cached_value]
    specs = [
        pl.BlockSpec((rows, HEAD_DIM), lambda h: (0, h)),
        column(groups),
        column(groups + 1),
        pl.BlockSpec((cached, HEAD_DIM), lambda h: (0, group)),
        pl.BlockSpec((cached, HEAD_DIM), lambda h: (0, group)),
    ]
    aliases = {}
    if earlier is not None:
        operands.append(earlier)
        specs.append(pl.BlockSpec(memory_space=pl.ANY))
        aliases = {5: 0}
    return pl.pallas_call(
        attend_kernel,
        grid=(groups,),
        out_shape=jax.ShapeDtypeStruct((rows, local_heads * groups * HEAD_DIM), jnp.bfloat16),
        in_specs=specs,
        out_specs=pl.BlockSpec((rows, HEAD_DIM), lambda h: (0, group * groups + h)),
        input_output_aliases=aliases,
        cost_estimate=pl.CostEstimate(
            flops=4 * groups * rows * (cached + rows) * HEAD_DIM,
            bytes_accessed=4 * groups * rows * HEAD_DIM,
            transcendentals=groups * rows * (cached + rows),
        ),
        compiler_params=pltpu.CompilerParams(vmem_limit_bytes=24 << 20),
        name="attend",
    )(*operands)


def fetch_blocks(kv_cache, selected):
    local_heads = kv_cache.shape[2] // HEAD_DIM
    devices = lax.axis_size("context")
    myself = lax.axis_index("context")
    owners = selected // BLOCKS_DEV
    offsets = selected % BLOCKS_DEV
    blocks = kv_cache.reshape(BLOCKS_DEV, C_BLOCK, 2, local_heads, HEAD_DIM)
    listings = devices * PICKS
    piece_rows = C_BLOCK // devices
    flat_owner = owners.reshape(listings)
    flat_offset = offsets.reshape(listings)
    serial = jnp.arange(listings, dtype=jnp.int32)
    earlier = (flat_owner[:, None] == flat_owner[None, :]) & (serial[:, None] > serial[None, :])
    ranks = jnp.sum(earlier.astype(jnp.int32), axis=1)
    slots = jnp.arange(MOST_REQ, dtype=jnp.int32)
    hits = (flat_owner[None, :] == myself) & (ranks[None, :] == slots[:, None])
    filled = jnp.any(hits, axis=1)
    picked = jnp.sum(jnp.where(hits, flat_offset[None, :], 0), axis=1)
    outbox = jnp.where(
        filled[:, None, None, None, None],
        jnp.take(blocks, picked, axis=0),
        jnp.zeros((), jnp.bfloat16),
    )
    outbox = outbox.reshape(MOST_REQ, devices, piece_rows, 2, local_heads, HEAD_DIM)
    spread = lax.all_to_all(outbox, "context", split_axis=1, concat_axis=1, tiled=True)
    relayed = spread.reshape(MOST_REQ * devices, piece_rows, 2, local_heads, HEAD_DIM)
    forward = jnp.take(relayed, ranks * devices + flat_owner, axis=0)
    forward = forward.reshape(devices, PICKS, piece_rows, 2, local_heads, HEAD_DIM)
    collected = lax.all_to_all(forward, "context", split_axis=0, concat_axis=2, tiled=True)
    fetched = collected[0]
    cached = fetched.shape[0] * fetched.shape[1]
    cached_key = fetched[:, :, 0].reshape(cached, local_heads * HEAD_DIM)
    cached_value = fetched[:, :, 1].reshape(cached, local_heads * HEAD_DIM)
    return cached_key, cached_value


def gather_features(hidden_in):
    if lax.axis_size("tensor") != 2:
        return lax.all_gather(hidden_in, "tensor", axis=1, tiled=True)
    other = lax.ppermute(hidden_in, "tensor", [(0, 1), (1, 0)])
    first = lax.axis_index("tensor") == 0
    return jnp.concatenate(
        [jnp.where(first, hidden_in, other), jnp.where(first, other, hidden_in)], axis=1
    )


def on_device(hidden_in, norm_gain, w_query, w_key, w_value, kv_cache, selected):
    local_heads = kv_cache.shape[2] // HEAD_DIM
    groups = w_query.shape[1] // (HEAD_DIM * local_heads)
    span = groups * HEAD_DIM
    weights = []
    for g in range(local_heads):
        stacked = jnp.concatenate(
            [
                w_query[:, g * span : (g + 1) * span],
                w_key[:, g * HEAD_DIM : (g + 1) * HEAD_DIM],
                w_value[:, g * HEAD_DIM : (g + 1) * HEAD_DIM],
            ],
            axis=1,
        )
        weights.append(lax.all_gather(stacked, "context", axis=0, tiled=True))
    gathered = gather_features(hidden_in)
    floats = gathered.astype(jnp.float32)
    inverse_rms = lax.rsqrt(jnp.mean(floats * floats, axis=1, keepdims=True) + 1e-05)
    normed = (floats * inverse_rms * norm_gain.astype(jnp.float32)).astype(jnp.bfloat16)
    normed = lax.optimization_barrier(normed)
    cached_key, cached_value = fetch_blocks(kv_cache, selected)
    result = None
    for g in range(local_heads):
        projected = jnp.dot(normed, weights[g], preferred_element_type=jnp.float32).astype(jnp.bfloat16)
        result = attend(projected, cached_key, cached_value, result, g, groups, local_heads)
    return result


def solution(mesh):
    return jax.shard_map(
        on_device,
        mesh=mesh,
        in_specs=(
            P("context", "tensor"),
            P(),
            P("context", "tensor"),
            P("context", "tensor"),
            P("context", "tensor"),
            P("context", None, "tensor"),
            P(),
        ),
        out_specs=P("context", "tensor"),
        check_vma=False,
    )
```

time: 271 us -> 320 us (1.18)
  waiting for transfers between devices: 170 us -> 204 us
  Pallas kernels: 0 us -> 23.6 us
  matrix products: 45.6 us -> 29.9 us
  other arithmetic: 8.76 us -> 13.9 us
    ppermute x0 -> x1, waiting for transfers between devices: none -> 46.5 us  [gather_features(): other = lax.ppermute(hidden_in, 'tensor', [(0, 1), (1, 0)])]
    pallas_call x0 -> x4, Pallas kernels: none -> 23.6 us  [attend(): pl.pallas_call(attend_kernel, grid=(groups,), out_shape=jax.ShapeDtypeStr...]
    all_to_all x2, waiting for transfers between devices: 56.9 us -> 36.3 us  [the longest x1 27.1 us: fetch_blocks(): lax.all_to_all(forward, 'context', split_axis=0, concat_axis=2, tiled=True)]
    sub x1 -> x0, matrix products: 12 us -> none  [on_device(): probs = jax.nn.softmax(scores, axis=-1).astype(jnp.bfloat16)]
    all_gather x2 -> x4, waiting for transfers between devices: 112 us -> 121 us  [on_device(): weights.append(lax.all_gather(stacked, 'context', axis=0, tiled=True))]
    reshape x7 -> x3, local copies, waits for them, and re-layouts: 12.8 us -> 5.13 us  [the longest x2 5.05 us: fetch_blocks(): blocks = kv_cache.reshape(BLOCKS_DEV, C_BLOCK, 2, local_heads, HEAD_DIM)]
    select_n x5 -> x6, other arithmetic: 1.29 us -> 5.2 us  [the longest x1 3.83 us: gather_features(): jnp.where(first, hidden_in, other)]
    dot_general x2 -> x4, matrix products: 33.6 us -> 29.9 us  [on_device(): jnp.dot(normed, weights[g], preferred_element_type=jnp.float32)]
  transfers between devices with their start and end apart: 4 -> 7, of which waited for: 3 -> 6; matrix products, arithmetic and copies ran while one was open for 8% -> 16% of each run, Pallas kernels for 0% -> 6%
where the time goes in v1:
time: 320 us; the launch traced here: 318 us
  waiting for transfers between devices  204 us (64%)
  matrix products  29.9 us (9%)
  Pallas kernels  23.6 us (7%)
  local copies, waits for them, and re-layouts  18.3 us (6%)
  starting transfers between devices  15.1 us (5%)
  other arithmetic  13.9 us (4%)
  between operations  13.4 us (4%)
    all_gather x4, waiting for transfers between devices, on_device(): weights.append(lax.all_gather(stacked, 'context', axis=0, tiled=True))  121 us
    ppermute x1, waiting for transfers between devices, gather_features(): other = lax.ppermute(hidden_in, 'tensor', [(0, 1), (1, 0)])  46.5 us
    dot_general x4, matrix products, on_device(): jnp.dot(normed, weights[g], preferred_element_type=jnp.float32)  29.9 us
    all_to_all x1, waiting for transfers between devices, fetch_blocks(): lax.all_to_all(forward, 'context', split_axis=0, concat_axis=2, tiled=True)  27.1 us
    pallas_call x4, Pallas kernels, attend(): pl.pallas_call(attend_kernel, grid=(groups,), out_shape=jax.ShapeDtypeStr...  23.6 us
    all_to_all x1, waiting for transfers between devices, fetch_blocks(): lax.all_to_all(outbox, 'context', split_axis=1, concat_axis=1, tiled=True)  9.23 us
    all_to_all x1, starting transfers between devices, fetch_blocks(): lax.all_to_all(forward, 'context', split_axis=0, concat_axis=2, tiled=True)  8.04 us
    all_to_all x1, starting transfers between devices, fetch_blocks(): lax.all_to_all(outbox, 'context', split_axis=1, concat_axis=1, tiled=True)  6.6 us
  transfers between devices with their start and end apart: 7, of which 6 were waited for; matrix products, arithmetic and copies ran while one was open for 16% of the time, Pallas kernels for 6%

profile of v1, /device:TPU:13, one launch (start us, length us, event | category | flops | bytes accessed | tf_op | source)
XLA Modules:
  0.0 318.3 jit_solution(9096239566457965081)
XLA Ops:
  6.5 0.0 all-gather.11.cloned.1.call-start
  6.5 1.3 fusion.11
  7.8 1.1 fusion.13
  9.0 0.8 pad_maximum_fusion.4
  9.7 0.0 all-gather.11.cloned.1.call-update
  9.8 0.0 all-gather.9.cloned.1.call-start
  9.8 0.8 pad_maximum_fusion.3
  10.6 0.0 all-gather.9.cloned.1.call-update
  10.7 0.0 all-gather.7.cloned.1.call-start
  10.7 0.8 pad_maximum_fusion.2
  11.5 0.0 all-gather.7.cloned.1.call-update
  11.5 0.0 all-gather.5.cloned.1.call-start
  11.6 0.8 pad_maximum_fusion.1
  12.4 0.0 all-gather.5.cloned.1.call-update
  12.4 0.0 copy-start.3
  12.4 3.2 reshape.111
  15.6 1.9 copy.69
  17.4 0.0 copy-done.3
  17.5 0.1 copy.64
  17.6 0.1 broadcast_in_dim.55
  17.6 0.1 eq.45
  17.7 0.2 convert_reduce_fusion
  17.9 0.1 select_reduce_fusion
  18.1 2.6 gather_fusion
  20.6 0.1 fusion.8
  20.8 0.0 copy-start.2
  20.8 0.2 fusion.3
  21.0 0.0 copy-start.1
  21.0 1.7 copy.70
  22.7 6.6 %all-to-all-start = ((bf16[6,16,8,2,4,128]{5,2,4,3,0,1:T(8,128)(2,1)}), bf16[6,16,8,2,4,128]{5,2,4,3,0,1:T(8,128)(2,1)}, u32[]{:S(2)}, u32[]{:S(2)}) async-start(bf16[6,16,8,2,4,128]{5,2,4,3,0,1:T(8,128)(2,1)} %copy.70), calls=%async_computation | async-start | bytes 3145728 | tf_op jit(solution)/shard_map/all_to_all | solution.py:103
  29.3 0.0 copy-done.1
  29.3 0.3 collective-permute-start
  29.6 0.1 reshape.94
  29.7 0.0 copy-done.2
  29.7 0.1 mul.48
  29.9 46.5 %collective-permute-done = bf16[512,2048]{1,0:T(8,128)(2,1)} collective-permute-done((bf16[512,2048]{1,0:T(8,128)(2,1)S(1)}, bf16[512,2048]{1,0:T(8,128)(2,1)}, u32[]{:S(2)}, u32[]{:S(2)}) %collective-permute-start) | collective-permute-done | bytes 2097184 | tf_op jit(solution)/shard_map/ppermute | solution.py:118
  76.3 3.8 %broadcast_select_fusion.1 = (bf16[512,2048]{1,0:T(8,128)(2,1)S(1)}, bf16[512,2048]{1,0:T(8,128)(2,1)}) fusion(bf16[512,2048]{1,0:T(8,128)(2,1)} %param.7, bf16[512,2048]{1,0:T(8,128)(2,1)} %collective-permute-done, pred[]{:T(512)S(6)} %eq.44), kind=kLoop, calls=%fused_computation.9 | loop fusion | flops 2097152 | bytes 8388609 | tf_op jit(solution)/shard_map/jit(_where)/select_n | solution.py:121
  80.2 9.2 %all-to-all-done = bf16[6,16,8,2,4,128]{5,2,4,3,0,1:T(8,128)(2,1)} async-done(((bf16[6,16,8,2,4,128]{5,2,4,3,0,1:T(8,128)(2,1)}), bf16[6,16,8,2,4,128]{5,2,4,3,0,1:T(8,128)(2,1)}, u32[]{:S(2)}, u32[]{:S(2)}) %all-to-all-start) | async-done | bytes 1572896 | tf_op jit(solution)/shard_map/all_to_all | solution.py:103
  89.4 3.0 copy.71
  92.4 2.2 gather_fusion.1
  94.6 1.1 broadcast_select_fusion.2
  95.7 8.0 %all-to-all-start.1 = ((bf16[16,3,8,2,4,128]{5,2,4,3,1,0:T(8,128)(2,1)}), bf16[16,3,8,2,4,128]{5,2,4,3,1,0:T(8,128)(2,1)S(1)}, u32[]{:S(2)}, u32[]{:S(2)}) async-start(bf16[16,3,8,2,4,128]{5,2,4,3,1,0:T(8,128)(2,1)} %broadcast_select_fusion.2), calls=%async_computation.1 | async-start | bytes 1572864 | tf_op jit(solution)/shard_map/all_to_all | solution.py:107
  103.7 0.0 copy-start
  103.8 2.4 fusion
  106.1 0.0 copy-done
  106.1 2.7 fusion.2
  108.9 27.1 %all-to-all-done.1 = bf16[16,3,8,2,4,128]{5,2,4,3,1,0:T(8,128)(2,1)S(1)} async-done(((bf16[16,3,8,2,4,128]{5,2,4,3,1,0:T(8,128)(2,1)}), bf16[16,3,8,2,4,128]{5,2,4,3,1,0:T(8,128)(2,1)S(1)}, u32[]{:S(2)}, u32[]{:S(2)}) %all-to-all-start.1) | async-done | bytes 786464 | tf_op jit(solution)/shard_map/all_to_all | solution.py:107
  135.9 0.2 copy_bitcast_fusion
  136.2 0.1 fusion.12
  136.2 0.3 copy.74
  136.5 0.3 copy.73
  136.9 0.1 copy_bitcast_fusion.1
  137.0 0.0 all-gather.11.cloned.1.call-done
  137.0 7.5 %convolution_convert_fusion.q_ref.k_ref.v_ref = bf16[512,768]{1,0:T(8,128)(2,1)S(1)} fusion(bf16[512,4096]{1,0:T(8,128)(2,1)} %fusion.2, bf16[4096,768]{1,0:T(8,128)(2,1)} %all-gather.11.cloned.1.call-done), kind=kOutput, calls=%fused_computation.12 | convolution fusion | flops 3221618688 | bytes 11272192 | tf_op jit(solution)/shard_map/dot_general | solution.py:148
  144.5 5.9 %attend.4.rest_0_ = bf16[512,2048]{1,0:T(8,128)(2,1)} custom-call(bf16[512,768]{1,0:T(8,128)(2,1)S(1)} %convolution_convert_fusion.q_ref.k_ref.v_ref, bf16[512,768]{1,0:T(8,128)(2,1)S(1)} %convolution_convert_fusion.q_ref.k_ref.v_ref, bf16[512,768]{1,0:T(8,128)(2,1)S(1)} %convolution_convert_fusion.q_ref.k_ref.v_ref, ...), custom_call_target="tpu_custom_call" | custom-call | flops 939524096 | bytes 1048576 | tf_op jit(solution)/shard_map/attend/pallas_call | solution.py:62
  150.4 22.6 %all-gather.9.cloned.1.call-done = bf16[4096,768]{1,0:T(8,128)(2,1)} async-done(((bf16[256,768]{1,0:T(8,128)(2,1)}), bf16[4096,768]{1,0:T(8,128)(2,1)}) %all-gather.9.cloned.1.call-update) | async-done | bytes 6291472 | tf_op jit(solution)/shard_map/all_gather | solution.py:139
  173.0 7.5 %convolution_convert_fusion.1.q_ref.k_ref.v_ref = bf16[512,768]{1,0:T(8,128)(2,1)S(1)} fusion(bf16[512,4096]{1,0:T(8,128)(2,1)} %fusion.2, bf16[4096,768]{1,0:T(8,128)(2,1)} %all-gather.9.cloned.1.call-done), kind=kOutput, calls=%fused_computation.13 | convolution fusion | flops 3221618688 | bytes 11272192 | tf_op jit(solution)/shard_map/dot_general | solution.py:148
  180.4 5.9 %attend.5.rest_0_ = bf16[512,2048]{1,0:T(8,128)(2,1)} custom-call(bf16[512,768]{1,0:T(8,128)(2,1)S(1)} %convolution_convert_fusion.1.q_ref.k_ref.v_ref, bf16[512,768]{1,0:T(8,128)(2,1)S(1)} %convolution_convert_fusion.1.q_ref.k_ref.v_ref, bf16[512,768]{1,0:T(8,128)(2,1)S(1)} %convolution_convert_fusion.1.q_ref.k_ref.v_ref, ...), custom_call_target="tpu_custom_call", output_to_operand_aliasing={{}: (5, {})} | custom-call | flops 939524096 | bytes 1048576 | tf_op jit(solution)/shard_map/attend/pallas_call | solution.py:62
  186.3 49.5 %all-gather.7.cloned.1.call-done = bf16[4096,768]{1,0:T(8,128)(2,1)} async-done(((bf16[256,768]{1,0:T(8,128)(2,1)}), bf16[4096,768]{1,0:T(8,128)(2,1)}) %all-gather.7.cloned.1.call-update) | async-done | bytes 6291472 | tf_op jit(solution)/shard_map/all_gather | solution.py:139
  235.8 7.5 %convolution_convert_fusion.2.q_ref.k_ref.v_ref = bf16[512,768]{1,0:T(8,128)(2,1)S(1)} fusion(bf16[512,4096]{1,0:T(8,128)(2,1)} %fusion.2, bf16[4096,768]{1,0:T(8,128)(2,1)} %all-gather.7.cloned.1.call-done), kind=kOutput, calls=%fused_computation.14 | convolution fusion | flops 3221618688 | bytes 11272192 | tf_op jit(solution)/shard_map/dot_general | solution.py:148
  243.3 5.9 %attend.6.rest_0_ = bf16[512,2048]{1,0:T(8,128)(2,1)} custom-call(bf16[512,768]{1,0:T(8,128)(2,1)S(1)} %convolution_convert_fusion.2.q_ref.k_ref.v_ref, bf16[512,768]{1,0:T(8,128)(2,1)S(1)} %convolution_convert_fusion.2.q_ref.k_ref.v_ref, bf16[512,768]{1,0:T(8,128)(2,1)S(1)} %convolution_convert_fusion.2.q_ref.k_ref.v_ref, ...), custom_call_target="tpu_custom_call", output_to_operand_aliasing={{}: (5, {})} | custom-call | flops 939524096 | bytes 1048576 | tf_op jit(solution)/shard_map/attend/pallas_call | solution.py:62
  249.2 49.2 %all-gather.5.cloned.1.call-done = bf16[4096,768]{1,0:T(8,128)(2,1)} async-done(((bf16[256,768]{1,0:T(8,128)(2,1)}), bf16[4096,768]{1,0:T(8,128)(2,1)}) %all-gather.5.cloned.1.call-update) | async-done | bytes 6291472 | tf_op jit(solution)/shard_map/all_gather | solution.py:139
  298.4 7.5 %convolution_convert_fusion.3.q_ref.k_ref.v_ref = bf16[512,768]{1,0:T(8,128)(2,1)S(1)} fusion(bf16[512,4096]{1,0:T(8,128)(2,1)} %fusion.2, bf16[4096,768]{1,0:T(8,128)(2,1)} %all-gather.5.cloned.1.call-done), kind=kOutput, calls=%fused_computation.15 | convolution fusion | flops 3221618688 | bytes 11272192 | tf_op jit(solution)/shard_map/dot_general | solution.py:148
  305.9 5.9 %attend.7 = bf16[512,2048]{1,0:T(8,128)(2,1)} custom-call(bf16[512,768]{1,0:T(8,128)(2,1)S(1)} %convolution_convert_fusion.3.q_ref.k_ref.v_ref, bf16[512,768]{1,0:T(8,128)(2,1)S(1)} %convolution_convert_fusion.3.q_ref.k_ref.v_ref, bf16[512,768]{1,0:T(8,128)(2,1)S(1)} %convolution_convert_fusion.3.q_ref.k_ref.v_ref, ...), custom_call_target="tpu_custom_call", output_to_operand_aliasing={{}: (5, {})} | custom-call | flops 939524096 | bytes 1048576 | tf_op jit(solution)/shard_map/attend/pallas_call | solution.py:62
  (11 shorter events, 0.1 us)
Async XLA Ops:
  6.5 130.5 %all-gather.11.cloned.1.call-start = ((), (), s32[]{:S(2)}) async-start(), calls=%async_computation.5 | async-start | bytes 6684672 | tf_op jit(solution)/shard_map/all_gather | solution.py:139
  9.8 163.2 %all-gather.9.cloned.1.call-start = ((), (), s32[]{:S(2)}) async-start(), calls=%async_computation.4 | async-start | bytes 6684672 | tf_op jit(solution)/shard_map/all_gather | solution.py:139
  10.7 225.2 %all-gather.7.cloned.1.call-start = ((), (), s32[]{:S(2)}) async-start(), calls=%async_computation.3 | async-start | bytes 6684672 | tf_op jit(solution)/shard_map/all_gather | solution.py:139
  11.5 286.9 %all-gather.5.cloned.1.call-start = ((), (), s32[]{:S(2)}) async-start(), calls=%async_computation.2 | async-start | bytes 6684672 | tf_op jit(solution)/shard_map/all_gather | solution.py:139
  12.4 5.1 %copy-start.3 = (s32[16,3]{0,1:T(4,128)S(1)}, s32[16,3]{0,1:T(4,128)}, u32[]{:S(2)}) copy-start(s32[16,3]{0,1:T(4,128)} %param.13) | copy-start | bytes 580
  20.8 8.9 %copy-start.2 = (bf16[4096]{0:T(1024)(128)(2,1)S(1)}, bf16[4096]{0:T(1024)(128)(2,1)}, u32[]{:S(2)}) copy-start(bf16[4096]{0:T(1024)(128)(2,1)} %param.8) | copy-start | bytes 24580
  21.0 8.3 %copy-start.1 = (bf16[512,2048]{1,0:T(8,128)(2,1)S(1)}, bf16[512,2048]{1,0:T(8,128)(2,1)}, u32[]{:S(2)}) copy-start(bf16[512,2048]{1,0:T(8,128)(2,1)} %param.7) | copy-start | bytes 6291460
  22.7 66.7 %all-to-all-start = ((bf16[6,16,8,2,4,128]{5,2,4,3,0,1:T(8,128)(2,1)}), bf16[6,16,8,2,4,128]{5,2,4,3,0,1:T(8,128)(2,1)}, u32[]{:S(2)}, u32[]{:S(2)}) async-start(bf16[6,16,8,2,4,128]{5,2,4,3,0,1:T(8,128)(2,1)} %copy.70), calls=%async_computation | async-start | bytes 3145728 | tf_op jit(solution)/shard_map/all_to_all | solution.py:103
  29.3 47.0 %collective-permute-start = (bf16[512,2048]{1,0:T(8,128)(2,1)S(1)}, bf16[512,2048]{1,0:T(8,128)(2,1)}, u32[]{:S(2)}, u32[]{:S(2)}) collective-permute-start(bf16[512,2048]{1,0:T(8,128)(2,1)S(1)} %copy-done.1), channel_id=1, source_target_pairs={{0,16},{16,0},{1,17},{17,1},{2,18},{18,2},{3,19},{19,3},{4,20},{20... | collective-permute-start | bytes 6291464 | tf_op jit(solution)/shard_map/ppermute | solution.py:118
  95.7 40.2 %all-to-all-start.1 = ((bf16[16,3,8,2,4,128]{5,2,4,3,1,0:T(8,128)(2,1)}), bf16[16,3,8,2,4,128]{5,2,4,3,1,0:T(8,128)(2,1)S(1)}, u32[]{:S(2)}, u32[]{:S(2)}) async-start(bf16[16,3,8,2,4,128]{5,2,4,3,1,0:T(8,128)(2,1)} %broadcast_select_fusion.2), calls=%async_computation.1 | async-start | bytes 1572864 | tf_op jit(solution)/shard_map/all_to_all | solution.py:107
  103.7 2.4 copy-start
Sparse Core Ops, SparseCore 0:
  9.9 84.4 all-gather.10
  96.7 76.2 all-gather.8
  175.3 60.4 all-gather.6
  237.9 60.4 all-gather.4

commit v2 on v1

--- a/solution.py
+++ b/solution.py
@@ -42,38 +42,31 @@
         o_ref[start:stop, :] = mixed.astype(o_ref.dtype)
 
 
-def attend(projected, cached_key, cached_value, earlier, group, groups, local_heads):
+def attend(projected, cached_key, cached_value, groups, local_heads):
     rows = projected.shape[0]
     cached = cached_key.shape[0]
-    column = lambda place: pl.BlockSpec((rows, HEAD_DIM), lambda h: (0, place))
-    operands = [projected, projected, projected, cached_key, cached_value]
-    specs = [
-        pl.BlockSpec((rows, HEAD_DIM), lambda h: (0, h)),
-        column(groups),
-        column(groups + 1),
-        pl.BlockSpec((cached, HEAD_DIM), lambda h: (0, group)),
-        pl.BlockSpec((cached, HEAD_DIM), lambda h: (0, group)),
-    ]
-    aliases = {}
-    if earlier is not None:
-        operands.append(earlier)
-        specs.append(pl.BlockSpec(memory_space=pl.ANY))
-        aliases = {5: 0}
+    heads = groups * local_heads
+    tall = lambda height, place: pl.BlockSpec((height, HEAD_DIM), lambda h: (0, place(h)))
     return pl.pallas_call(
         attend_kernel,
-        grid=(groups,),
-        out_shape=jax.ShapeDtypeStruct((rows, local_heads * groups * HEAD_DIM), jnp.bfloat16),
-        in_specs=specs,
-        out_specs=pl.BlockSpec((rows, HEAD_DIM), lambda h: (0, group * groups + h)),
-        input_output_aliases=aliases,
+        grid=(heads,),
+        out_shape=jax.ShapeDtypeStruct((rows, heads * HEAD_DIM), jnp.bfloat16),
+        in_specs=[
+            tall(rows, lambda h: h),
+            tall(rows, lambda h: heads + h // groups),
+            tall(rows, lambda h: heads + local_heads + h // groups),
+            tall(cached, lambda h: h // groups),
+            tall(cached, lambda h: h // groups),
+        ],
+        out_specs=tall(rows, lambda h: h),
         cost_estimate=pl.CostEstimate(
-            flops=4 * groups * rows * (cached + rows) * HEAD_DIM,
-            bytes_accessed=4 * groups * rows * HEAD_DIM,
-            transcendentals=groups * rows * (cached + rows),
+            flops=4 * heads * rows * (cached + rows) * HEAD_DIM,
+            bytes_accessed=4 * heads * rows * HEAD_DIM,
+            transcendentals=heads * rows * (cached + rows),
         ),
         compiler_params=pltpu.CompilerParams(vmem_limit_bytes=24 << 20),
         name="attend",
-    )(*operands)
+    )(projected, projected, projected, cached_key, cached_value)
 
 
 def fetch_blocks(kv_cache, selected):
@@ -125,29 +118,16 @@
 def on_device(hidden_in, norm_gain, w_query, w_key, w_value, kv_cache, selected):
     local_heads = kv_cache.shape[2] // HEAD_DIM
     groups = w_query.shape[1] // (HEAD_DIM * local_heads)
-    span = groups * HEAD_DIM
-    weights = []
-    for g in range(local_heads):
-        stacked = jnp.concatenate(
-            [
-                w_query[:, g * span : (g + 1) * span],
-                w_key[:, g * HEAD_DIM : (g + 1) * HEAD_DIM],
-                w_value[:, g * HEAD_DIM : (g + 1) * HEAD_DIM],
-            ],
-            axis=1,
-        )
-        weights.append(lax.all_gather(stacked, "context", axis=0, tiled=True))
+    stacked = jnp.concatenate([w_query, w_key, w_value], axis=1)
+    weights = lax.all_gather(stacked, "context", axis=0, tiled=True)
     gathered = gather_features(hidden_in)
     floats = gathered.astype(jnp.float32)
     inverse_rms = lax.rsqrt(jnp.mean(floats * floats, axis=1, keepdims=True) + 1e-05)
     normed = (floats * inverse_rms * norm_gain.astype(jnp.float32)).astype(jnp.bfloat16)
     normed = lax.optimization_barrier(normed)
     cached_key, cached_value = fetch_blocks(kv_cache, selected)
-    result = None
-    for g in range(local_heads):
-        projected = jnp.dot(normed, weights[g], preferred_element_type=jnp.float32).astype(jnp.bfloat16)
-        result = attend(projected, cached_key, cached_value, result, g, groups, local_heads)
-    return result
+    projected = jnp.dot(normed, weights, preferred_element_type=jnp.float32).astype(jnp.bfloat16)
+    return attend(projected, cached_key, cached_value, groups, local_heads)
 
 
 def solution(mesh):

time: 320 us -> 238 us (0.74)
  waiting for transfers between devices: 204 us -> 140 us
  matrix products: 29.9 us -> 18.1 us
    all_gather x4 -> x1, waiting for transfers between devices: 121 us -> 68.8 us  [on_device(): weights = lax.all_gather(stacked, 'context', axis=0, tiled=True)]
    dot_general x4 -> x1, matrix products: 29.9 us -> 18.1 us  [on_device(): jnp.dot(normed, weights, preferred_element_type=jnp.float32)]
    all_to_all x1, waiting for transfers between devices: 9.23 us -> 2.23 us  [fetch_blocks(): lax.all_to_all(outbox, 'context', split_axis=1, concat_axis=1, tiled=True)]
    all_to_all x1, waiting for transfers between devices: 27.1 us -> 22.5 us  [fetch_blocks(): lax.all_to_all(forward, 'context', split_axis=0, concat_axis=2, tiled=True)]
    pallas_call x4 -> x1, Pallas kernels: 23.6 us -> 22.2 us  [attend(): pl.pallas_call(attend_kernel, grid=(heads,), out_shape=jax.ShapeDtypeStru...]
  transfers between devices with their start and end apart: 7 -> 4, of which waited for: 6 -> 4; matrix products, arithmetic and copies ran while one was open for 16% -> 11% of each run, Pallas kernels for 6% -> 0%
where the time goes in v2:
time: 238 us; the launch traced here: 237 us
  waiting for transfers between devices  140 us (59%)
  Pallas kernels  22.2 us (9%)
  matrix products  18.1 us (8%)
  local copies, waits for them, and re-layouts  15.7 us (7%)
  starting transfers between devices  14.3 us (6%)
  other arithmetic  13.6 us (6%)
  between operations  13.6 us (6%)
    all_gather x1, waiting for transfers between devices, on_device(): weights = lax.all_gather(stacked, 'context', axis=0, tiled=True)  68.8 us
    ppermute x1, waiting for transfers between devices, gather_features(): other = lax.ppermute(hidden_in, 'tensor', [(0, 1), (1, 0)])  46.5 us
    all_to_all x1, waiting for transfers between devices, fetch_blocks(): lax.all_to_all(forward, 'context', split_axis=0, concat_axis=2, tiled=True)  22.5 us
    pallas_call x1, Pallas kernels, attend(): pl.pallas_call(attend_kernel, grid=(heads,), out_shape=jax.ShapeDtypeStru...  22.2 us
    dot_general x1, matrix products, on_device(): jnp.dot(normed, weights, preferred_element_type=jnp.float32)  18.1 us
    all_to_all x1, starting transfers between devices, fetch_blocks(): lax.all_to_all(forward, 'context', split_axis=0, concat_axis=2, tiled=True)  7.25 us
    all_to_all x1, starting transfers between devices, fetch_blocks(): lax.all_to_all(outbox, 'context', split_axis=1, concat_axis=1, tiled=True)  6.71 us
    reshape x2, local copies, waits for them, and re-layouts, fetch_blocks(): blocks = kv_cache.reshape(BLOCKS_DEV, C_BLOCK, 2, local_heads, HEAD_DIM)  5.05 us
  transfers between devices with their start and end apart: 4, of which 4 were waited for; matrix products, arithmetic and copies ran while one was open for 11% of the time, Pallas kernels for 0%

profile of v2, /device:TPU:13, one launch (start us, length us, event | category | flops | bytes accessed | tf_op | source)
XLA Modules:
  0.0 237.3 jit_solution(9989686536397820239)
XLA Ops:
  6.5 0.0 all-gather.2.cloned.1.call-start
  6.5 2.8 %pad_maximum_fusion.1 = bf16[256,3072]{1,0:T(8,128)(2,1)} fusion(bf16[256,512]{1,0:T(8,128)(2,1)} %param.11, bf16[256,512]{1,0:T(8,128)(2,1)} %param.10, bf16[256,2048]{1,0:T(8,128)(2,1)} %param.9), kind=kLoop, calls=%fused_computation.11 | loop fusion | flops 4718592 | bytes 3145728 | tf_op jit(solution)/shard_map/concatenate | solution.py:121
  9.3 0.0 all-gather.2.cloned.1.call-update
  9.3 3.2 %reshape.111 = bf16[8,128,2,4,128]{4,3,2,1,0:T(4,128)(2,1)S(1)} reshape(bf16[1024,2,512]{2,1,0:T(2,128)(2,1)} %param.12) | data formatting | bytes 4194304 | tf_op jit(solution)/shard_map/reshape | solution.py:78
  12.5 0.0 copy-start.3
  12.5 1.9 copy.66
  14.4 0.0 copy-done.3
  14.4 0.1 copy.61
  14.5 0.1 broadcast_in_dim.55
  14.6 0.1 eq.45
  14.7 0.2 convert_reduce_fusion
  14.9 0.1 select_reduce_fusion
  15.0 2.4 %gather_fusion = bf16[6,128,2,4,128]{4,1,3,2,0:T(8,128)(2,1)S(1)} fusion(bf16[8,128,2,4,128]{4,1,3,2,0:T(8,128)(2,1)} %copy.66, s32[1024]{0:T(1024)S(1)} %pad_clamp_fusion.1), kind=kCustom, calls=%fused_computation | custom fusion | bytes 3145752 | tf_op jit(solution)/shard_map/jit(_take)/gather | solution.py:92
  17.5 0.1 fusion.8
  17.6 0.2 fusion.3
  17.8 1.6 copy.67
  19.5 0.0 copy-start.1
  19.5 0.0 copy-start.2
  19.5 6.7 %all-to-all-start = ((bf16[6,16,8,2,4,128]{5,2,4,3,0,1:T(8,128)(2,1)}), bf16[6,16,8,2,4,128]{5,2,4,3,0,1:T(8,128)(2,1)}, u32[]{:S(2)}, u32[]{:S(2)}) async-start(bf16[6,16,8,2,4,128]{5,2,4,3,0,1:T(8,128)(2,1)} %copy.67), calls=%async_computation | async-start | bytes 3145728 | tf_op jit(solution)/shard_map/all_to_all | solution.py:96
  26.2 0.0 copy-done.1
  26.2 0.3 collective-permute-start
  26.5 0.1 reshape.94
  26.6 0.0 copy-done.2
  26.6 0.1 mul.48
  26.8 46.5 %collective-permute-done = bf16[512,2048]{1,0:T(8,128)(2,1)} collective-permute-done((bf16[512,2048]{1,0:T(8,128)(2,1)S(1)}, bf16[512,2048]{1,0:T(8,128)(2,1)}, u32[]{:S(2)}, u32[]{:S(2)}) %collective-permute-start) | collective-permute-done | bytes 2097184 | tf_op jit(solution)/shard_map/ppermute | solution.py:111
  73.2 3.8 %broadcast_select_fusion.1 = (bf16[512,2048]{1,0:T(8,128)(2,1)S(1)}, bf16[512,2048]{1,0:T(8,128)(2,1)}) fusion(bf16[512,2048]{1,0:T(8,128)(2,1)} %param.7, bf16[512,2048]{1,0:T(8,128)(2,1)} %collective-permute-done, pred[]{:T(512)S(6)} %eq.44), kind=kLoop, calls=%fused_computation.10 | loop fusion | flops 2097152 | bytes 8388609 | tf_op jit(solution)/shard_map/jit(_where)/select_n | solution.py:114
  77.1 2.2 all-to-all-done
  79.3 3.0 %copy.68 = bf16[6,16,8,2,4,128]{5,2,4,3,1,0:T(8,128)(2,1)} copy(bf16[6,16,8,2,4,128]{5,2,4,3,0,1:T(8,128)(2,1)} %all-to-all-done) | data formatting | bytes 3145728 | tf_op jit(solution)/shard_map/all_to_all | solution.py:96
  82.3 2.1 gather_fusion.1
  84.4 1.1 broadcast_select_fusion.2
  85.4 7.3 %all-to-all-start.1 = ((bf16[16,3,8,2,4,128]{5,2,4,3,1,0:T(8,128)(2,1)}), bf16[16,3,8,2,4,128]{5,2,4,3,1,0:T(8,128)(2,1)S(1)}, u32[]{:S(2)}, u32[]{:S(2)}) async-start(bf16[16,3,8,2,4,128]{5,2,4,3,1,0:T(8,128)(2,1)} %broadcast_select_fusion.2), calls=%async_computation.1 | async-start | bytes 1572864 | tf_op jit(solution)/shard_map/all_to_all | solution.py:100
  92.7 0.0 copy-start
  92.7 2.4 %fusion = f32[512]{0:T(512)S(1)} fusion(bf16[512,2048]{1,0:T(8,128)(2,1)} %get-tuple-element.6, bf16[512,2048]{1,0:T(8,128)(2,1)S(1)} %get-tuple-element.5), kind=kLoop, calls=%fused_computation.4 | loop fusion | flops 12582400 | bytes 4196352 | tf_op jit(solution)/shard_map/reduce_sum | solution.py:125
  95.1 0.0 copy-done
  95.1 2.8 %fusion.2 = bf16[512,4096]{1,0:T(8,128)(2,1)} fusion(f32[4096]{0:T(1024)S(1)} %convert_element_type.16, f32[512]{0:T(512)S(1)} %add_rsqrt_fusion, bf16[512,2048]{1,0:T(8,128)(2,1)S(1)} %copy-done, bf16[512,2048]{1,0:T(8,128)(2,1)S(1)} %get-tuple-element.5), kind=kLoop, calls=%fused_computation.6 | loop fusion | flops 14680064 | bytes 8407040 | tf_op jit(solution)/shard_map/convert_element_type | solution.py:126
  97.9 22.5 %all-to-all-done.1 = bf16[16,3,8,2,4,128]{5,2,4,3,1,0:T(8,128)(2,1)S(1)} async-done(((bf16[16,3,8,2,4,128]{5,2,4,3,1,0:T(8,128)(2,1)}), bf16[16,3,8,2,4,128]{5,2,4,3,1,0:T(8,128)(2,1)S(1)}, u32[]{:S(2)}, u32[]{:S(2)}) %all-to-all-start.1) | async-done | bytes 786464 | tf_op jit(solution)/shard_map/all_to_all | solution.py:100
  120.4 0.2 copy_bitcast_fusion
  120.6 0.1 fusion.11
  120.7 0.3 copy.71
  121.0 0.3 copy.70
  121.3 0.1 copy_bitcast_fusion.1
  121.4 68.8 %all-gather.2.cloned.1.call-done = bf16[4096,3072]{1,0:T(8,128)(2,1)} async-done(((bf16[256,3072]{1,0:T(8,128)(2,1)}), bf16[4096,3072]{1,0:T(8,128)(2,1)}) %all-gather.2.cloned.1.call-update) | async-done | bytes 25165840 | tf_op jit(solution)/shard_map/all_gather | solution.py:122
  190.2 18.1 %convolution_convert_fusion.q_ref.k_ref.v_ref = bf16[512,3072]{1,0:T(8,128)(2,1)S(1)} fusion(bf16[512,4096]{1,0:T(8,128)(2,1)} %fusion.2, bf16[4096,3072]{1,0:T(8,128)(2,1)} %all-gather.2.cloned.1.call-done), kind=kOutput, calls=%fused_computation.7 | convolution fusion | flops 12886474752 | bytes 32505856 | tf_op jit(solution)/shard_map/dot_general | solution.py:129
  208.3 22.2 %attend.1 = bf16[512,2048]{1,0:T(8,128)(2,1)} custom-call(bf16[512,3072]{1,0:T(8,128)(2,1)S(1)} %convolution_convert_fusion.q_ref.k_ref.v_ref, bf16[512,3072]{1,0:T(8,128)(2,1)S(1)} %convolution_convert_fusion.q_ref.k_ref.v_ref, bf16[512,3072]{1,0:T(8,128)(2,1)S(1)} %convolution_convert_fusion.q_ref.k_ref.v_ref, ...), custom_call_target="tpu_custom_call" | custom-call | flops 3758096384 | bytes 4194304 | tf_op jit(solution)/shard_map/attend/pallas_call | solution.py:50
  (11 shorter events, 0.1 us)
Async XLA Ops:
  6.5 183.7 %all-gather.2.cloned.1.call-start = ((), (), s32[]{:S(2)}) async-start(), calls=%async_computation.2 | async-start | bytes 26738688 | tf_op jit(solution)/shard_map/all_gather | solution.py:122
  12.5 1.9 copy-start.3
  19.5 6.7 %copy-start.1 = (bf16[512,2048]{1,0:T(8,128)(2,1)S(1)}, bf16[512,2048]{1,0:T(8,128)(2,1)}, u32[]{:S(2)}) copy-start(bf16[512,2048]{1,0:T(8,128)(2,1)} %param.7) | copy-start | bytes 6291460
  19.5 7.1 %copy-start.2 = (bf16[4096]{0:T(1024)(128)(2,1)S(1)}, bf16[4096]{0:T(1024)(128)(2,1)}, u32[]{:S(2)}) copy-start(bf16[4096]{0:T(1024)(128)(2,1)} %param.8) | copy-start | bytes 24580
  19.5 59.8 %all-to-all-start = ((bf16[6,16,8,2,4,128]{5,2,4,3,0,1:T(8,128)(2,1)}), bf16[6,16,8,2,4,128]{5,2,4,3,0,1:T(8,128)(2,1)}, u32[]{:S(2)}, u32[]{:S(2)}) async-start(bf16[6,16,8,2,4,128]{5,2,4,3,0,1:T(8,128)(2,1)} %copy.67), calls=%async_computation | async-start | bytes 3145728 | tf_op jit(solution)/shard_map/all_to_all | solution.py:96
  26.2 47.0 %collective-permute-start = (bf16[512,2048]{1,0:T(8,128)(2,1)S(1)}, bf16[512,2048]{1,0:T(8,128)(2,1)}, u32[]{:S(2)}, u32[]{:S(2)}) collective-permute-start(bf16[512,2048]{1,0:T(8,128)(2,1)S(1)} %copy-done.1), channel_id=1, source_target_pairs={{0,16},{16,0},{1,17},{17,1},{2,18},{18,2},{3,19},{19,3},{4,20},{20... | collective-permute-start | bytes 6291464 | tf_op jit(solution)/shard_map/ppermute | solution.py:111
  85.4 34.9 %all-to-all-start.1 = ((bf16[16,3,8,2,4,128]{5,2,4,3,1,0:T(8,128)(2,1)}), bf16[16,3,8,2,4,128]{5,2,4,3,1,0:T(8,128)(2,1)S(1)}, u32[]{:S(2)}, u32[]{:S(2)}) async-start(bf16[16,3,8,2,4,128]{5,2,4,3,1,0:T(8,128)(2,1)} %broadcast_select_fusion.2), calls=%async_computation.1 | async-start | bytes 1572864 | tf_op jit(solution)/shard_map/all_to_all | solution.py:100
  92.7 2.4 %copy-start = (bf16[512,2048]{1,0:T(8,128)(2,1)S(1)}, bf16[512,2048]{1,0:T(8,128)(2,1)}, u32[]{:S(2)}) copy-start(bf16[512,2048]{1,0:T(8,128)(2,1)} %get-tuple-element.6) | copy-start | bytes 6291460
Sparse Core Ops, SparseCore 0:
  9.4 180.7 all-gather.1

commit v3 on v2

--- a/solution.py
+++ b/solution.py
@@ -1,3 +1,4 @@
+import functools
 import math
 
 import jax
@@ -15,50 +16,58 @@
 ROW_TILE = 256
 
 
-def attend_kernel(q_ref, k_ref, v_ref, ck_ref, cv_ref, *rest):
-    o_ref = rest[-1]
+def attend_kernel(groups, q_ref, k_ref, v_ref, ck_ref, cv_ref, o_ref):
     rows = q_ref.shape[0]
-    scale = 1.0 / math.sqrt(HEAD_DIM)
+    tile = min(ROW_TILE, rows)
+    factor = math.log2(math.e) / math.sqrt(HEAD_DIM)
     dims = (((1,), (1,)), ((), ()))
-    for start in range(0, rows, ROW_TILE):
-        stop = start + ROW_TILE
-        query = q_ref[start:stop, :]
-        cached = lax.dot_general(query, ck_ref[...], dims, preferred_element_type=jnp.float32) * scale
-        fresh = lax.dot_general(query, k_ref[:stop, :], dims, preferred_element_type=jnp.float32) * scale
-        row = lax.broadcasted_iota(jnp.int32, fresh.shape, 0) + start
-        col = lax.broadcasted_iota(jnp.int32, fresh.shape, 1)
-        fresh = jnp.where(col <= row, fresh, -jnp.inf)
-        top = jnp.maximum(jnp.max(cached, axis=1, keepdims=True), jnp.max(fresh, axis=1, keepdims=True))
-        cached = jnp.exp(cached - top)
-        fresh = jnp.exp(fresh - top)
-        total = jnp.sum(cached, axis=1, keepdims=True) + jnp.sum(fresh, axis=1, keepdims=True)
-        inverse = 1.0 / total
-        mixed = jnp.dot(
-            (cached * inverse).astype(jnp.bfloat16), cv_ref[...], preferred_element_type=jnp.float32
-        )
-        mixed += jnp.dot(
-            (fresh * inverse).astype(jnp.bfloat16), v_ref[:stop, :], preferred_element_type=jnp.float32
-        )
-        o_ref[start:stop, :] = mixed.astype(o_ref.dtype)
+    for head in range(groups):
+        place = slice(head * HEAD_DIM, (head + 1) * HEAD_DIM)
+        for start in range(0, rows, tile):
+            stop = start + tile
+            query = q_ref[start:stop, place]
+            cached = lax.dot_general(query, ck_ref[...], dims, preferred_element_type=jnp.float32)
+            fresh = lax.dot_general(query, k_ref[:stop, :], dims, preferred_element_type=jnp.float32)
+            row = lax.broadcasted_iota(jnp.int32, fresh.shape, 0) + start
+            col = lax.broadcasted_iota(jnp.int32, fresh.shape, 1)
+            fresh = jnp.where(col <= row, fresh, -jnp.inf)
+            top = jnp.maximum(
+                jnp.max(cached, axis=1, keepdims=True), jnp.max(fresh, axis=1, keepdims=True)
+            )
+            cached = jnp.exp2((cached - top) * factor)
+            fresh = jnp.exp2((fresh - top) * factor)
+            total = jnp.sum(cached, axis=1, keepdims=True) + jnp.sum(fresh, axis=1, keepdims=True)
+            inverse = 1.0 / total
+            mixed = jnp.dot(
+                (cached * inverse).astype(jnp.bfloat16),
+                cv_ref[...],
+                preferred_element_type=jnp.float32,
+            )
+            mixed += jnp.dot(
+                (fresh * inverse).astype(jnp.bfloat16),
+                v_ref[:stop, :],
+                preferred_element_type=jnp.float32,
+            )
+            o_ref[start:stop, place] = mixed.astype(o_ref.dtype)
 
 
 def attend(projected, cached_key, cached_value, groups, local_heads):
     rows = projected.shape[0]
     cached = cached_key.shape[0]
     heads = groups * local_heads
-    tall = lambda height, place: pl.BlockSpec((height, HEAD_DIM), lambda h: (0, place(h)))
+    block = lambda height, width, place: pl.BlockSpec((height, width), lambda g: (0, place(g)))
     return pl.pallas_call(
-        attend_kernel,
-        grid=(heads,),
+        functools.partial(attend_kernel, groups),
+        grid=(local_heads,),
         out_shape=jax.ShapeDtypeStruct((rows, heads * HEAD_DIM), jnp.bfloat16),
         in_specs=[
-            tall(rows, lambda h: h),
-            tall(rows, lambda h: heads + h // groups),
-            tall(rows, lambda h: heads + local_heads + h // groups),
-            tall(cached, lambda h: h // groups),
-            tall(cached, lambda h: h // groups),
+            block(rows, groups * HEAD_DIM, lambda g: g),
+            block(rows, HEAD_DIM, lambda g: heads + g),
+            block(rows, HEAD_DIM, lambda g: heads + local_heads + g),
+            block(cached, HEAD_DIM, lambda g: g),
+            block(cached, HEAD_DIM, lambda g: g),
         ],
-        out_specs=tall(rows, lambda h: h),
+        out_specs=block(rows, groups * HEAD_DIM, lambda g: g),
         cost_estimate=pl.CostEstimate(
             flops=4 * heads * rows * (cached + rows) * HEAD_DIM,
             bytes_accessed=4 * heads * rows * HEAD_DIM,
@@ -67,6 +76,167 @@
         compiler_params=pltpu.CompilerParams(vmem_limit_bytes=24 << 20),
         name="attend",
     )(projected, projected, projected, cached_key, cached_value)
+
+
+def project_kernel(chips, cores, n_ref, w_ref, o_ref, held, total, copy_sem, ring_send, ring_recv, pair_send, pair_recv):
+    me = lax.axis_index("context")
+    core = lax.rem(me, cores)
+    chip = me // cores
+    length = chips // 2
+
+    def place_to_chip(place):
+        side = place // length
+        along = (1 - side) * place + side * (chips - 1 - place)
+        return 2 * along + side
+
+    side = lax.rem(chip, 2)
+    along = chip // 2
+    spot = (1 - side) * along + side * (chips - 1 - along)
+    right = place_to_chip(lax.rem(spot + 1, chips)) * cores + core
+    left = place_to_chip(lax.rem(spot + chips - 1, chips)) * cores + core
+    sibling = chip * cores + (cores - 1 - core)
+    partners = [right, left] + ([sibling] if cores == 2 else [])
+
+    own = [
+        pltpu.make_async_copy(w_ref.at[way], held.at[way, chip, core], copy_sem.at[way])
+        for way in range(2)
+    ]
+    for copy in own:
+        copy.start()
+    barrier = pltpu.get_barrier_semaphore()
+    for partner in partners:
+        pl.semaphore_signal(
+            barrier, inc=1, device_id={"context": partner}, device_id_type=pl.DeviceIdType.MESH
+        )
+    pl.semaphore_wait(barrier, len(partners))
+    total[...] = jnp.zeros_like(total)
+    for copy in own:
+        copy.wait()
+
+    def origin(way, step):
+        return place_to_chip(lax.rem(spot + (chips - step if way == 0 else step), chips))
+
+    def ring(way, step):
+        piece = held.at[way, origin(way, step), core]
+        return pltpu.make_async_remote_copy(
+            src_ref=piece,
+            dst_ref=piece,
+            send_sem=ring_send.at[way, step],
+            recv_sem=ring_recv.at[way, step],
+            device_id={"context": right if way == 0 else left},
+            device_id_type=pl.DeviceIdType.MESH,
+        )
+
+    def arrived(way, step):
+        piece = held.at[way, origin(way, step), core]
+        return pltpu.make_async_remote_copy(
+            src_ref=piece,
+            dst_ref=piece,
+            send_sem=ring_send.at[way, step - 1],
+            recv_sem=ring_recv.at[way, step - 1],
+            device_id={"context": right if way == 0 else left},
+            device_id_type=pl.DeviceIdType.MESH,
+        )
+
+    def pair(way, step, from_core):
+        piece = held.at[way, origin(way, step), from_core]
+        return pltpu.make_async_remote_copy(
+            src_ref=piece,
+            dst_ref=piece,
+            send_sem=pair_send.at[way, step],
+            recv_sem=pair_recv.at[way, step],
+            device_id={"context": sibling},
+            device_id_type=pl.DeviceIdType.MESH,
+        )
+
+    half = held.shape[4]
+    depth = cores * held.shape[3]
+    width = 256 if half % 256 == 0 else 128
+
+    def compute(way, step):
+        if cores == 2:
+            pair(way, step, 1 - core).wait_recv()
+        source = origin(way, step)
+
+        def tile(t, carry):
+            cols = pl.ds(pl.multiple_of(t * width, width), width)
+            block = held[way, source, :, :, cols].reshape(depth, width)
+            total[way, :, cols] += jnp.dot(n_ref[source], block, preferred_element_type=jnp.float32)
+            return carry
+
+        lax.fori_loop(0, half // width, tile, 0)
+
+    for way in range(2):
+        ring(way, 0).start()
+        if cores == 2:
+            pair(way, 0, core).start()
+
+    def body(step, carry):
+        for way in range(2):
+            arrived(way, step).wait_recv()
+
+            @pl.when(step < chips - 1)
+            def _():
+                ring(way, step).start()
+
+            if cores == 2:
+                pair(way, step, core).start()
+        for way in range(2):
+            compute(way, step - 1)
+        return carry
+
+    lax.fori_loop(1, chips, body, 0)
+    for way in range(2):
+        compute(way, chips - 1)
+        for begin in range(0, half, width):
+            o_ref[:, way * half + begin : way * half + begin + width] = total[
+                way, :, begin : begin + width
+            ].astype(o_ref.dtype)
+
+    def drain(step, carry):
+        for way in range(2):
+
+            @pl.when(step < chips - 1)
+            def _():
+                ring(way, step).wait_send()
+
+            if cores == 2:
+                pair(way, step, core).wait_send()
+        return carry
+
+    lax.fori_loop(0, chips, drain, 0)
+
+
+def project(normed, stacked):
+    devices = lax.axis_size("context")
+    cores = 2 if lax.axis_size("tensor") == 2 else 1
+    chips = devices // cores
+    rows = normed.shape[0]
+    depth, columns = stacked.shape
+    half = columns // 2
+    split = jnp.stack([stacked[:, :half], stacked[:, half:]])
+    return pl.pallas_call(
+        functools.partial(project_kernel, chips, cores),
+        out_shape=jax.ShapeDtypeStruct((rows, columns), jnp.bfloat16),
+        in_specs=[
+            pl.BlockSpec(memory_space=pltpu.VMEM),
+            pl.BlockSpec(memory_space=pl.ANY),
+        ],
+        out_specs=pl.BlockSpec(memory_space=pltpu.VMEM),
+        scratch_shapes=[
+            pltpu.VMEM((2, chips, cores, depth, half), jnp.bfloat16),
+            pltpu.VMEM((2, rows, half), jnp.float32),
+            pltpu.SemaphoreType.DMA((2,)),
+            pltpu.SemaphoreType.DMA((2, chips)),
+            pltpu.SemaphoreType.DMA((2, chips)),
+            pltpu.SemaphoreType.DMA((2, chips)),
+            pltpu.SemaphoreType.DMA((2, chips)),
+        ],
+        compiler_params=pltpu.CompilerParams(
+            collective_id=0, has_side_effects=True, vmem_limit_bytes=52 << 20
+        ),
+        name="project",
+    )(normed.reshape(rows, chips, cores * depth).transpose(1, 0, 2), split)
 
 
 def fetch_blocks(kv_cache, selected):
@@ -119,14 +289,13 @@
     local_heads = kv_cache.shape[2] // HEAD_DIM
     groups = w_query.shape[1] // (HEAD_DIM * local_heads)
     stacked = jnp.concatenate([w_query, w_key, w_value], axis=1)
-    weights = lax.all_gather(stacked, "context", axis=0, tiled=True)
     gathered = gather_features(hidden_in)
     floats = gathered.astype(jnp.float32)
     inverse_rms = lax.rsqrt(jnp.mean(floats * floats, axis=1, keepdims=True) + 1e-05)
     normed = (floats * inverse_rms * norm_gain.astype(jnp.float32)).astype(jnp.bfloat16)
-    normed = lax.optimization_barrier(normed)
     cached_key, cached_value = fetch_blocks(kv_cache, selected)
-    projected = jnp.dot(normed, weights, preferred_element_type=jnp.float32).astype(jnp.bfloat16)
+    normed, cached_key, cached_value = lax.optimization_barrier((normed, cached_key, cached_value))
+    projected = project(normed, stacked)
     return attend(projected, cached_key, cached_value, groups, local_heads)
 
 

time: 238 us -> 272 us (1.14); the launches traced: 237 us -> 267 us
  Pallas kernels: 22.2 us -> 153 us
  waiting for transfers between devices: 140 us -> 57.5 us
  matrix products: 18.1 us -> 0 us
  between operations: 13.6 us -> 0.27 us
  local copies, waits for them, and re-layouts: 15.7 us -> 27.9 us
    pallas_call x1 -> x2, Pallas kernels: 22.2 us -> 153 us  [the longest x1 134 us: project(): pl.pallas_call(functools.partial(project_kernel, chips, cores), out_shape...]
    all_gather x1 -> x0, waiting for transfers between devices: 68.8 us -> none  [on_device(): weights = lax.all_gather(stacked, 'context', axis=0, tiled=True)]
    dot_general x1 -> x0, matrix products: 18.1 us -> none  [on_device(): jnp.dot(normed, weights, preferred_element_type=jnp.float32)]
    all_to_all x1, waiting for transfers between devices: 22.5 us -> 11.1 us  [fetch_blocks(): lax.all_to_all(forward, 'context', split_axis=0, concat_axis=2, tiled=True)]
    unnamed x9 -> x16, local copies, waits for them, and re-layouts: 0.1 us -> 7.25 us
    reshape x0 -> x1, local copies, waits for them, and re-layouts: none -> 6.54 us  [project(): normed.reshape(rows, chips, cores * depth).transpose(1, 0, 2)]
    concatenate x1 -> x0, other arithmetic: 2.76 us -> none  [on_device(): stacked = jnp.concatenate([w_query, w_key, w_value], axis=1)]
  transfers between devices with their start and end apart: 4 -> 3, of which waited for: 4 -> 2; matrix products, arithmetic and copies ran while one was open for 11% -> 6% of each run, Pallas kernels for 0% -> 0%
where the time goes in v3:
time: 272 us; the launch traced here: 267 us
  Pallas kernels  153 us (56%)
  waiting for transfers between devices  57.5 us (21%)
  local copies, waits for them, and re-layouts  27.9 us (10%)
  other arithmetic  14.5 us (5%)
  starting transfers between devices  13.7 us (5%)
    pallas_call x1, Pallas kernels, project(): pl.pallas_call(functools.partial(project_kernel, chips, cores), out_shape...  134 us
    ppermute x1, waiting for transfers between devices, gather_features(): other = lax.ppermute(hidden_in, 'tensor', [(0, 1), (1, 0)])  46.4 us
    pallas_call x1, Pallas kernels, attend(): pl.pallas_call(functools.partial(attend_kernel, groups), grid=(local_head...  18.7 us
    all_to_all x1, waiting for transfers between devices, fetch_blocks(): lax.all_to_all(forward, 'context', split_axis=0, concat_axis=2, tiled=True)  11.1 us
    unnamed x16, local copies, waits for them, and re-layouts  7.25 us
    all_to_all x1, starting transfers between devices, fetch_blocks(): lax.all_to_all(forward, 'context', split_axis=0, concat_axis=2, tiled=True)  6.85 us
    all_to_all x1, starting transfers between devices, fetch_blocks(): lax.all_to_all(outbox, 'context', split_axis=1, concat_axis=1, tiled=True)  6.58 us
    reshape x1, local copies, waits for them, and re-layouts, project(): normed.reshape(rows, chips, cores * depth).transpose(1, 0, 2)  6.54 us
  transfers between devices with their start and end apart: 3, of which 2 were waited for; matrix products, arithmetic and copies ran while one was open for 6% of the time, Pallas kernels for 0%

profile of v3, /device:TPU:13, one launch (start us, length us, event | category | flops | bytes accessed | tf_op | source)
XLA Modules:
  0.0 266.6 jit_solution(12646582990009390100)
XLA Ops:
  0.0 0.8 copy.88
  0.8 0.1 eq.45
  0.9 0.2 convert_reduce_fusion
  1.1 0.1 broadcast_in_dim.55
  1.1 0.1 select_reduce_fusion
  1.3 0.1 fusion.9
  1.4 3.2 %reshape.115 = bf16[8,128,2,4,128]{4,3,2,1,0:T(4,128)(2,1)S(1)} reshape(bf16[1024,2,512]{2,1,0:T(2,128)(2,1)} %param.12) | data formatting | bytes 4194304 | tf_op jit(solution)/shard_map/reshape | solution.py:248
  4.6 1.9 copy.93
  6.5 2.4 gather_fusion
  8.9 0.2 fusion.3
  9.2 1.6 copy.94
  10.8 6.6 %all-to-all-start = ((bf16[6,16,8,2,4,128]{5,2,4,3,0,1:T(8,128)(2,1)}), bf16[6,16,8,2,4,128]{5,2,4,3,0,1:T(8,128)(2,1)S(1)}, u32[]{:S(2)}, u32[]{:S(2)}) async-start(bf16[6,16,8,2,4,128]{5,2,4,3,0,1:T(8,128)(2,1)} %copy.94), calls=%async_computation | async-start | bytes 3145728 | tf_op jit(solution)/shard_map/all_to_all | solution.py:266
  17.4 0.0 copy-start.6
  17.4 0.0 copy-start.3
  17.4 0.0 copy-start.4
  17.4 0.0 copy-start.5
  17.4 4.0 %copy.86 = bf16[512,2048]{0,1:T(8,128)(2,1)} copy(bf16[512,2048]{1,0:T(8,128)(2,1)} %param.7) | data formatting | bytes 4194304 | tf_op args[0]
  21.5 0.2 collective-permute-start
  21.7 0.1 reshape.97
  21.8 0.1 mul.48
  21.9 0.0 copy-done.6
  21.9 0.0 copy-done.3
  22.0 0.0 copy-done.4
  22.0 0.0 copy-done.5
  22.0 0.1 slice_bitcast_fusion
  22.1 0.1 pad_maximum_fusion.1.w_ref
  22.3 46.4 %collective-permute-done = bf16[512,2048]{0,1:T(8,128)(2,1)} collective-permute-done((bf16[512,2048]{0,1:T(8,128)(2,1)}, bf16[512,2048]{0,1:T(8,128)(2,1)}, u32[]{:S(2)}, u32[]{:S(2)}) %collective-permute-start) | collective-permute-done | bytes 2097184 | tf_op jit(solution)/shard_map/ppermute | solution.py:281
  68.6 4.5 %broadcast_select_fusion.1 = (bf16[512,2048]{0,1:T(8,128)(2,1)}, bf16[512,2048]{0,1:T(8,128)(2,1)}) fusion(bf16[512,2048]{0,1:T(8,128)(2,1)} %copy.86, bf16[512,2048]{0,1:T(8,128)(2,1)} %collective-permute-done, pred[]{:T(512)S(6)} %eq.44), kind=kLoop, calls=%fused_computation.9 | loop fusion | flops 2097152 | bytes 8388609 | tf_op jit(solution)/shard_map/jit(_where)/select_n | solution.py:284
  73.2 0.0 all-to-all-done
  73.2 1.5 copy.95
  74.7 2.1 gather_fusion.1
  76.8 1.0 broadcast_select_fusion.2
  77.8 6.8 %all-to-all-start.1 = ((bf16[16,3,8,2,4,128]{5,2,4,3,1,0:T(8,128)(2,1)}), bf16[16,3,8,2,4,128]{5,2,4,3,1,0:T(8,128)(2,1)S(1)}, u32[]{:S(2)}, u32[]{:S(2)}) async-start(bf16[16,3,8,2,4,128]{5,2,4,3,1,0:T(8,128)(2,1)} %broadcast_select_fusion.2), calls=%async_computation.1 | async-start | bytes 1572864 | tf_op jit(solution)/shard_map/all_to_all | solution.py:270
  84.7 0.0 copy-start.1
  84.7 0.0 copy-start.2
  84.7 2.9 %fusion = f32[512]{0:T(512)S(1)} fusion(bf16[512,2048]{0,1:T(8,128)(2,1)} %get-tuple-element.12, bf16[512,2048]{0,1:T(8,128)(2,1)} %get-tuple-element.11), kind=kLoop, calls=%fused_computation.4 | loop fusion | flops 12582400 | bytes 4196352 | tf_op jit(solution)/shard_map/reduce_sum | solution.py:294
  87.6 0.0 copy-done.1
  87.6 0.5 copy-done.2
  88.2 5.0 %fusion.2 = bf16[512,4096]{0,1:T(8,128)(2,1)} fusion(f32[4096]{0:T(1024)S(1)} %convert_element_type.13, f32[512]{0:T(512)S(1)} %add_rsqrt_fusion, bf16[512,2048]{0,1:T(8,128)(2,1)S(1)} %copy-done.2, bf16[512,2048]{0,1:T(8,128)(2,1)S(1)} %copy-done.1), kind=kLoop, calls=%fused_computation.6 | loop fusion | flops 14680064 | bytes 8407040 | tf_op jit(solution)/shard_map/convert_element_type | solution.py:295
  93.2 11.1 %all-to-all-done.1 = bf16[16,3,8,2,4,128]{5,2,4,3,1,0:T(8,128)(2,1)S(1)} async-done(((bf16[16,3,8,2,4,128]{5,2,4,3,1,0:T(8,128)(2,1)}), bf16[16,3,8,2,4,128]{5,2,4,3,1,0:T(8,128)(2,1)S(1)}, u32[]{:S(2)}, u32[]{:S(2)}) %all-to-all-start.1) | async-done | bytes 786464 | tf_op jit(solution)/shard_map/all_to_all | solution.py:270
  104.2 0.2 copy_bitcast_fusion
  104.5 0.1 fusion.12
  104.5 0.3 copy.97
  104.8 0.3 copy.98
  105.2 0.1 copy_bitcast_fusion.1
  105.3 6.5 %copy.99 = bf16[512,8,512]{2,0,1:T(8,128)(2,1)} copy(bf16[512,8,512]{0,2,1:T(8,128)(2,1)} %bitcast.39) | data formatting | bytes 8388608 | tf_op jit(solution)/shard_map/reshape | solution.py:239
  111.8 134.2 %project.1.q_ref.k_ref.v_ref = bf16[512,3072]{1,0:T(8,128)(2,1)} custom-call(bf16[8,512,512]{2,1,0:T(8,128)(2,1)} %bitcast.40, bf16[2,256,1536]{2,1,0:T(8,128)(2,1)S(1)} %pad_maximum_fusion.1.w_ref), custom_call_target="tpu_custom_call" | custom-call | tf_op jit(solution)/shard_map/project/pallas_call | solution.py:218
  246.1 0.0 copy-start
  246.1 1.9 copy-done
  248.0 18.7 %attend.1 = bf16[512,2048]{1,0:T(8,128)(2,1)} custom-call(bf16[512,3072]{1,0:T(8,128)(2,1)S(1)} %copy-done, bf16[512,3072]{1,0:T(8,128)(2,1)S(1)} %copy-done, bf16[512,3072]{1,0:T(8,128)(2,1)S(1)} %copy-done, bf16[384,512]{1,0:T(8,128)(2,1)S(1)} %get-tuple-element.9.ck_ref, bf16[384,512]{1,0:T(8,128)(2,1)S(1)} %get-tuple-element.10.cv_ref), custom_call_target="tpu_custom_call" | custom-call | flops 3758096384 | bytes 4194304 | tf_op jit(solution)/shard_map/attend/pallas_call | solution.py:59
  (11 shorter events, 0.1 us)
Async XLA Ops:
  10.8 62.4 %all-to-all-start = ((bf16[6,16,8,2,4,128]{5,2,4,3,0,1:T(8,128)(2,1)}), bf16[6,16,8,2,4,128]{5,2,4,3,0,1:T(8,128)(2,1)S(1)}, u32[]{:S(2)}, u32[]{:S(2)}) async-start(bf16[6,16,8,2,4,128]{5,2,4,3,0,1:T(8,128)(2,1)} %copy.94), calls=%async_computation | async-start | bytes 3145728 | tf_op jit(solution)/shard_map/all_to_all | solution.py:266
  17.4 4.5 %copy-start.6 = (bf16[4096]{0:T(1024)(128)(2,1)S(1)}, bf16[4096]{0:T(1024)(128)(2,1)}, u32[]{:S(2)}) copy-start(bf16[4096]{0:T(1024)(128)(2,1)} %param.8) | copy-start | bytes 24580
  17.4 4.6 %copy-start.3 = (bf16[256,2048]{1,0:T(8,128)(2,1)S(1)}, bf16[256,2048]{1,0:T(8,128)(2,1)}, u32[]{:S(2)}) copy-start(bf16[256,2048]{1,0:T(8,128)(2,1)} %param.9) | copy-start | bytes 3145732
  17.4 4.6 %copy-start.4 = (bf16[256,512]{1,0:T(8,128)(2,1)S(1)}, bf16[256,512]{1,0:T(8,128)(2,1)}, u32[]{:S(2)}) copy-start(bf16[256,512]{1,0:T(8,128)(2,1)} %param.11) | copy-start | bytes 786436
  17.4 4.6 %copy-start.5 = (bf16[256,512]{1,0:T(8,128)(2,1)S(1)}, bf16[256,512]{1,0:T(8,128)(2,1)}, u32[]{:S(2)}) copy-start(bf16[256,512]{1,0:T(8,128)(2,1)} %param.10) | copy-start | bytes 786436
  21.5 47.2 %collective-permute-start = (bf16[512,2048]{0,1:T(8,128)(2,1)}, bf16[512,2048]{0,1:T(8,128)(2,1)}, u32[]{:S(2)}, u32[]{:S(2)}) collective-permute-start(bf16[512,2048]{0,1:T(8,128)(2,1)} %copy.86), channel_id=1, source_target_pairs={{0,16},{16,0},{1,17},{17,1},{2,18},{18,2},{3,19},{19,3},{4,20},{20... | collective-permute-start | bytes 6291464 | tf_op jit(solution)/shard_map/ppermute | solution.py:281
  77.8 26.4 %all-to-all-start.1 = ((bf16[16,3,8,2,4,128]{5,2,4,3,1,0:T(8,128)(2,1)}), bf16[16,3,8,2,4,128]{5,2,4,3,1,0:T(8,128)(2,1)S(1)}, u32[]{:S(2)}, u32[]{:S(2)}) async-start(bf16[16,3,8,2,4,128]{5,2,4,3,1,0:T(8,128)(2,1)} %broadcast_select_fusion.2), calls=%async_computation.1 | async-start | bytes 1572864 | tf_op jit(solution)/shard_map/all_to_all | solution.py:270
  84.7 2.9 %copy-start.1 = (bf16[512,2048]{0,1:T(8,128)(2,1)S(1)}, bf16[512,2048]{0,1:T(8,128)(2,1)}, u32[]{:S(2)}) copy-start(bf16[512,2048]{0,1:T(8,128)(2,1)} %get-tuple-element.11) | copy-start | bytes 6291460
  84.7 3.5 %copy-start.2 = (bf16[512,2048]{0,1:T(8,128)(2,1)S(1)}, bf16[512,2048]{0,1:T(8,128)(2,1)}, u32[]{:S(2)}) copy-start(bf16[512,2048]{0,1:T(8,128)(2,1)} %get-tuple-element.12) | copy-start | bytes 6291460
  246.1 1.9 copy-start

commit v4 on v3

v4 whole, which is shorter than its diff:
```python
import functools
import math

import jax
import jax.numpy as jnp
from jax import lax
from jax.experimental import pallas as pl
from jax.experimental.pallas import tpu as pltpu
from jax.sharding import PartitionSpec as P

HEAD_DIM = 128
C_BLOCK = 128
PICKS = 3
MOST_REQ = 6
BLOCKS_DEV = 8
ROW_TILE = 256


def attend_kernel(groups, q_ref, k_ref, v_ref, ck_ref, cv_ref, o_ref):
    rows = q_ref.shape[0]
    tile = min(ROW_TILE, rows)
    factor = math.log2(math.e) / math.sqrt(HEAD_DIM)
    dims = (((1,), (1,)), ((), ()))
    for head in range(groups):
        place = slice(head * HEAD_DIM, (head + 1) * HEAD_DIM)
        for start in range(0, rows, tile):
            stop = start + tile
            query = q_ref[start:stop, place]
            cached = lax.dot_general(query, ck_ref[...], dims, preferred_element_type=jnp.float32)
            fresh = lax.dot_general(query, k_ref[:stop, :], dims, preferred_element_type=jnp.float32)
            row = lax.broadcasted_iota(jnp.int32, fresh.shape, 0) + start
            col = lax.broadcasted_iota(jnp.int32, fresh.shape, 1)
            fresh = jnp.where(col <= row, fresh, -jnp.inf)
            top = jnp.maximum(
                jnp.max(cached, axis=1, keepdims=True), jnp.max(fresh, axis=1, keepdims=True)
            )
            cached = jnp.exp2((cached - top) * factor)
            fresh = jnp.exp2((fresh - top) * factor)
            total = jnp.sum(cached, axis=1, keepdims=True) + jnp.sum(fresh, axis=1, keepdims=True)
            inverse = 1.0 / total
            mixed = jnp.dot(
                (cached * inverse).astype(jnp.bfloat16),
                cv_ref[...],
                preferred_element_type=jnp.float32,
            )
            mixed += jnp.dot(
                (fresh * inverse).astype(jnp.bfloat16),
                v_ref[:stop, :],
                preferred_element_type=jnp.float32,
            )
            o_ref[start:stop, place] = mixed.astype(o_ref.dtype)


def attend(projected, cached_key, cached_value, groups, local_heads):
    rows = projected.shape[0]
    cached = cached_key.shape[0]
    heads = groups * local_heads
    block = lambda height, width, place: pl.BlockSpec((height, width), lambda g: (0, place(g)))
    return pl.pallas_call(
        functools.partial(attend_kernel, groups),
        grid=(local_heads,),
        out_shape=jax.ShapeDtypeStruct((rows, heads * HEAD_DIM), jnp.bfloat16),
        in_specs=[
            block(rows, groups * HEAD_DIM, lambda g: g),
            block(rows, HEAD_DIM, lambda g: heads + g),
            block(rows, HEAD_DIM, lambda g: heads + local_heads + g),
            block(cached, HEAD_DIM, lambda g: g),
            block(cached, HEAD_DIM, lambda g: g),
        ],
        out_specs=block(rows, groups * HEAD_DIM, lambda g: g),
        cost_estimate=pl.CostEstimate(
            flops=4 * heads * rows * (cached + rows) * HEAD_DIM,
            bytes_accessed=4 * heads * rows * HEAD_DIM,
            transcendentals=heads * rows * (cached + rows),
        ),
        compiler_params=pltpu.CompilerParams(vmem_limit_bytes=24 << 20),
        name="attend",
    )(projected, projected, projected, cached_key, cached_value)


def project_kernel(
    chips, cores, picks_ref, owner_ref, rank_ref, gain_ref, kv_ref, h_ref, w_ref, o_ref, f_ref,
    held, total, hidden, normed, outbox, inbox, forward, copy_sem, ring_send, ring_recv,
    pair_send, pair_recv, peer_send, peer_recv, spread_send, spread_recv, last_send, last_recv,
):
    mesh_id = pl.DeviceIdType.MESH
    me = lax.axis_index("context")
    devices = lax.axis_size("context")
    mine = lax.axis_index("tensor")
    peers = lax.axis_size("tensor")
    core = lax.rem(me, cores)
    chip = me // cores
    length = chips // 2

    def place_to_chip(place):
        side = place // length
        along = (1 - side) * place + side * (chips - 1 - place)
        return 2 * along + side

    side = lax.rem(chip, 2)
    along = chip // 2
    spot = (1 - side) * along + side * (chips - 1 - along)
    right = place_to_chip(lax.rem(spot + 1, chips)) * cores + core
    left = place_to_chip(lax.rem(spot + chips - 1, chips)) * cores + core
    sibling = chip * cores + (cores - 1 - core)

    own = [
        pltpu.make_async_copy(w_ref.at[way], held.at[way, chip, core], copy_sem.at[way])
        for way in range(2)
    ]
    own.append(pltpu.make_async_copy(h_ref, hidden.at[mine], copy_sem.at[2]))
    for copy in own:
        copy.start()
    barrier = pltpu.get_barrier_semaphore()

    def greet(k, carry):
        pl.semaphore_signal(
            barrier, inc=1, device_id={"context": lax.rem(me + k, devices)}, device_id_type=mesh_id
        )
        return carry

    lax.fori_loop(1, devices, greet, 0)
    for k in range(1, peers):
        pl.semaphore_signal(
            barrier, inc=1, device_id={"tensor": lax.rem(mine + k, peers)}, device_id_type=mesh_id
        )
    pl.semaphore_wait(barrier, devices - 1 + peers - 1)
    for copy in own:
        copy.wait()

    def origin(way, step):
        return place_to_chip(lax.rem(spot + (chips - step if way == 0 else step), chips))

    def ring(way, step, sem):
        piece = held.at[way, origin(way, step), core]
        return pltpu.make_async_remote_copy(
            src_ref=piece,
            dst_ref=piece,
            send_sem=ring_send.at[way, sem],
            recv_sem=ring_recv.at[way, sem],
            device_id={"context": right if way == 0 else left},
            device_id_type=mesh_id,
        )

    def pair(way, step, from_core):
        piece = held.at[way, origin(way, step), from_core]
        return pltpu.make_async_remote_copy(
            src_ref=piece,
            dst_ref=piece,
            send_sem=pair_send.at[way, step],
            recv_sem=pair_recv.at[way, step],
            device_id={"context": sibling},
            device_id_type=mesh_id,
        )

    def peer(k, slot):
        return pltpu.make_async_remote_copy(
            src_ref=hidden.at[slot],
            dst_ref=hidden.at[slot],
            send_sem=peer_send.at[k],
            recv_sem=peer_recv.at[k],
            device_id={"tensor": lax.rem(mine + k, peers)},
            device_id_type=mesh_id,
        )

    def spread(k, slot):
        return pltpu.make_async_remote_copy(
            src_ref=outbox.at[lax.rem(me + k, devices)],
            dst_ref=inbox.at[slot],
            send_sem=spread_send.at[k],
            recv_sem=spread_recv.at[k],
            device_id={"context": lax.rem(me + k, devices)},
            device_id_type=mesh_id,
        )

    def last(k, slot):
        return pltpu.make_async_remote_copy(
            src_ref=forward.at[lax.rem(me + k, devices)],
            dst_ref=f_ref.at[slot],
            send_sem=last_send.at[k],
            recv_sem=last_recv.at[k],
            device_id={"context": lax.rem(me + k, devices)},
            device_id_type=mesh_id,
        )

    def loop(begin, end, action):
        def run(k, carry):
            action(k)
            return carry

        lax.fori_loop(begin, end, run, 0)

    for k in range(1, peers):
        peer(k, mine).start()
    for way in range(2):
        ring(way, 0, 0).start()
        if cores == 2:
            pair(way, 0, core).start()

    def fill(slot):
        outbox[:, slot] = kv_ref[picks_ref[slot]]

    loop(0, MOST_REQ, fill)
    loop(1, devices, lambda k: spread(k, me).start())
    kept = pltpu.make_async_copy(outbox.at[me], inbox.at[me], copy_sem.at[3])
    kept.start()
    total[...] = jnp.zeros_like(total)

    half = held.shape[4]
    depth = cores * held.shape[3]
    width = 256 if half % 256 == 0 else 128

    def compute(way, step):
        if cores == 2:
            pair(way, step, 1 - core).wait_recv()
        source = origin(way, step)

        def tile(t):
            cols = pl.ds(pl.multiple_of(t * width, width), width)
            block = held[way, source, :, :, cols].reshape(depth, width)
            total[way, :, cols] += jnp.dot(normed[source], block, preferred_element_type=jnp.float32)

        loop(0, half // width, tile)

    def advance(step):
        for way in range(2):
            ring(way, step, step - 1).wait_recv()

            @pl.when(step < chips - 1)
            def _():
                ring(way, step, step).start()

            if cores == 2:
                pair(way, step, core).start()

    loop(1, length - 1, advance)
    for k in range(1, peers):
        peer(k, lax.rem(mine + peers - k, peers)).wait_recv()
    rows = hidden.shape[1]
    part = hidden.shape[2]
    height = min(64, rows)

    def normalise(t):
        at = pl.ds(pl.multiple_of(t * height, height), height)
        squares = jnp.zeros((height, 1), jnp.float32)
        for slot in range(peers):
            floats = hidden[slot, at, :].astype(jnp.float32)
            squares += jnp.sum(floats * floats, axis=1, keepdims=True)
        inverse = lax.rsqrt(squares / (peers * part) + 1e-05)
        for source in range(chips):
            slot, begin = source * depth // part, source * depth % part
            floats = hidden[slot, at, begin : begin + depth].astype(jnp.float32)
            gain = gain_ref[:, source * depth : (source + 1) * depth].astype(jnp.float32)
            normed[source, at, :] = (floats * inverse * gain).astype(jnp.bfloat16)

    loop(0, rows // height, normalise)
    advance(length - 1)
    loop(1, devices, lambda k: spread(k, lax.rem(me + devices - k, devices)).wait_recv())
    kept.wait()

    def relay(listing):
        forward[listing // PICKS, lax.rem(listing, PICKS)] = inbox[
            owner_ref[listing], rank_ref[listing]
        ]

    loop(0, devices * PICKS, relay)
    loop(1, devices, lambda k: last(k, me).start())
    kept_last = pltpu.make_async_copy(forward.at[me], f_ref.at[me], copy_sem.at[4])
    kept_last.start()

    def second(step):
        advance(step)
        for early in range(2):
            for way in range(2):
                compute(way, (step - length) * 2 + early)

    loop(length, chips, second)
    for way in range(2):
        for begin in range(0, half, width):
            o_ref[:, way * half + begin : way * half + begin + width] = total[
                way, :, begin : begin + width
            ].astype(o_ref.dtype)
    loop(1, devices, lambda k: last(k, lax.rem(me + devices - k, devices)).wait_recv())
    kept_last.wait()

    def drain(step):
        for way in range(2):

            @pl.when(step < chips - 1)
            def _():
                ring(way, step, step).wait_send()

            if cores == 2:
                pair(way, step, core).wait_send()

    loop(0, chips, drain)
    loop(1, devices, lambda k: spread(k, me).wait_send())
    loop(1, devices, lambda k: last(k, me).wait_send())
    for k in range(1, peers):
        peer(k, mine).wait_send()


def project(hidden_in, norm_gain, stacked, kv_cache, picked, owners, ranks):
    devices = lax.axis_size("context")
    peers = lax.axis_size("tensor")
    cores = 2 if peers == 2 else 1
    chips = devices // cores
    rows, part = hidden_in.shape
    depth, columns = stacked.shape
    half = columns // 2
    span = kv_cache.shape[2]
    piece = C_BLOCK // devices
    split = jnp.stack([stacked[:, :half], stacked[:, half:]])
    smem = pl.BlockSpec(memory_space=pltpu.SMEM)
    vmem = pl.BlockSpec(memory_space=pltpu.VMEM)
    anywhere = pl.BlockSpec(memory_space=pl.ANY)
    sems = lambda *shape: pltpu.SemaphoreType.DMA(shape)
    return pl.pallas_call(
        functools.partial(project_kernel, chips, cores),
        out_shape=(
            jax.ShapeDtypeStruct((rows, columns), jnp.bfloat16),
            jax.ShapeDtypeStruct((devices, PICKS, piece, 2, span), jnp.bfloat16),
        ),
        in_specs=[smem, smem, smem, vmem, vmem, anywhere, anywhere],
        out_specs=(vmem, vmem),
        scratch_shapes=[
            pltpu.VMEM((2, chips, cores, depth, half), jnp.bfloat16),
            pltpu.VMEM((2, rows, half), jnp.float32),
            pltpu.VMEM((peers, rows, part), jnp.bfloat16),
            pltpu.VMEM((chips, rows, cores * depth), jnp.bfloat16),
            pltpu.VMEM((devices, MOST_REQ, piece, 2, span), jnp.bfloat16),
            pltpu.VMEM((devices, MOST_REQ, piece, 2, span), jnp.bfloat16),
            pltpu.VMEM((devices, PICKS, piece, 2, span), jnp.bfloat16),
            sems(5),
            sems(2, chips),
            sems(2, chips),
            sems(2, chips),
            sems(2, chips),
            sems(peers),
            sems(peers),
            sems(devices),
            sems(devices),
            sems(devices),
            sems(devices),
        ],
        compiler_params=pltpu.CompilerParams(
            collective_id=0, has_side_effects=True, vmem_limit_bytes=58 << 20
        ),
        name="project",
    )(
        picked,
        owners,
        ranks,
        norm_gain.reshape(1, -1),
        kv_cache.reshape(BLOCKS_DEV, devices, piece, 2, span),
        hidden_in,
        split,
    )


def on_device(hidden_in, norm_gain, w_query, w_key, w_value, kv_cache, selected):
    local_heads = kv_cache.shape[2] // HEAD_DIM
    groups = w_query.shape[1] // (HEAD_DIM * local_heads)
    devices = lax.axis_size("context")
    stacked = jnp.concatenate([w_query, w_key, w_value], axis=1)
    owners = (selected // BLOCKS_DEV).reshape(devices * PICKS)
    offsets = (selected % BLOCKS_DEV).reshape(devices * PICKS)
    serial = jnp.arange(devices * PICKS, dtype=jnp.int32)
    earlier = (owners[:, None] == owners[None, :]) & (serial[:, None] > serial[None, :])
    ranks = jnp.sum(earlier.astype(jnp.int32), axis=1)
    slots = jnp.arange(MOST_REQ, dtype=jnp.int32)
    hits = (owners[None, :] == lax.axis_index("context")) & (ranks[None, :] == slots[:, None])
    picked = jnp.sum(jnp.where(hits, offsets[None, :], 0), axis=1)
    projected, fetched = project(hidden_in, norm_gain, stacked, kv_cache, picked, owners, ranks)
    fetched = fetched.transpose(1, 0, 2, 3, 4).reshape(PICKS * C_BLOCK, 2, kv_cache.shape[2])
    return attend(projected, fetched[:, 0], fetched[:, 1], groups, local_heads)


def solution(mesh):
    return jax.shard_map(
        on_device,
        mesh=mesh,
        in_specs=(
            P("context", "tensor"),
            P(),
            P("context", "tensor"),
            P("context", "tensor"),
            P("context", "tensor"),
            P("context", None, "tensor"),
            P(),
        ),
        out_specs=P("context", "tensor"),
        check_vma=False,
    )
```

time: 272 us -> 218 us (0.80)
  waiting for transfers between devices: 57.5 us -> 0 us
  Pallas kernels: 153 us -> 206 us
  local copies, waits for them, and re-layouts: 27.9 us -> 3.76 us
  starting transfers between devices: 13.7 us -> 0 us
  other arithmetic: 14.5 us -> 4.27 us
    pallas_call x1, Pallas kernels: 134 us -> 187 us  [project(): pl.pallas_call(functools.partial(project_kernel, chips, cores), out_shape...]
    ppermute x1 -> x0, waiting for transfers between devices: 46.4 us -> none  [gather_features(): other = lax.ppermute(hidden_in, 'tensor', [(0, 1), (1, 0)])]
    all_to_all x2 -> x0, starting transfers between devices: 13.4 us -> none  [the longest x1 6.85 us: fetch_blocks(): lax.all_to_all(forward, 'context', split_axis=0, concat_axis=2, tiled=True)]
    all_to_all x2 -> x0, waiting for transfers between devices: 11.1 us -> none  [the longest x1 11.1 us: fetch_blocks(): lax.all_to_all(forward, 'context', split_axis=0, concat_axis=2, tiled=True)]
    reshape x4 -> x1, local copies, waits for them, and re-layouts: 11.7 us -> 1.3 us  [project(): norm_gain.reshape(1, -1)]
    unnamed x16 -> x6, local copies, waits for them, and re-layouts: 7.25 us -> 0.69 us
    select_n x6 -> x1, other arithmetic: 5.82 us -> 0.69 us  [on_device(): owners = (selected // BLOCKS_DEV).reshape(devices * PICKS)]
    convert_element_type x2 -> x0, other arithmetic: 4.99 us -> none  [the longest x1 4.98 us: on_device(): (floats * inverse_rms * norm_gain.astype(jnp.float32)).astype(jnp.bfloat16)]
  transfers between devices with their start and end apart: 3 -> 0, of which waited for: 2 -> 0; matrix products, arithmetic and copies ran while one was open for 6% -> 0% of each run, Pallas kernels for 0% -> 0%
where the time goes in v4:
time: 218 us; the launch traced here: 214 us
  Pallas kernels  206 us (94%)
  other arithmetic  4.27 us (2%)
  local copies, waits for them, and re-layouts  3.76 us (2%)
    pallas_call x1, Pallas kernels, project(): pl.pallas_call(functools.partial(project_kernel, chips, cores), out_shape...  187 us
    pallas_call x1, Pallas kernels, attend(): pl.pallas_call(functools.partial(attend_kernel, groups), grid=(local_head...  18.7 us

profile of v4, /device:TPU:13, one launch (start us, length us, event | category | flops | bytes accessed | tf_op | source)
XLA Modules:
  0.0 214.0 jit_solution(18387866980647321077)
XLA Ops:
  0.0 0.7 add_select_fusion.1
  0.7 0.1 copy.14
  0.8 0.1 broadcast_in_dim_reshape.2.owner_ref
  0.9 0.0 copy-start.1
  0.9 0.2 convert_reduce_fusion.rank_ref
  1.1 0.0 copy-start.2
  1.1 0.1 copy.15
  1.2 0.1 broadcast_in_dim.18
  1.2 0.7 select_reduce_fusion.picks_ref
  1.9 1.3 reshape.21.gain_ref
  3.2 1.4 slice_bitcast_fusion
  4.7 0.0 copy-done.1
  4.7 0.0 copy-done.2
  4.7 1.3 pad_maximum_fusion.w_ref
  6.0 187.2 %project.1 = (bf16[512,3072]{1,0:T(8,128)(2,1)}, bf16[16,3,8,2,512]{4,3,2,1,0:T(2,128)(2,1)}) custom-call(s32[6]{0:T(128)} %select_reduce_fusion.picks_ref, s32[48]{0:T(128)} %copy-done.1, s32[48]{0:T(128)} %copy-done.2, bf16[1,4096]{1,0:T(2,128)(2,1)} %reshape.21.gain_ref, bf16[8,16,8,2,512]{4,3,2,1,0:T(2,128)(2,1)} %bitcast.12, bf16[512,2048]{1,0:T(8,128)(2,1)} %h_ref.1, ...), custom_call_target="tpu_custom_call" | custom-call | tf_op jit(solution)/shard_map/project/pallas_call | solution.py:318
  193.2 0.0 copy-start
  193.2 1.4 copy.16
  194.6 0.1 slice_bitcast_fusion.1
  194.7 0.7 copy-done
  195.4 18.7 %attend.1 = bf16[512,2048]{1,0:T(8,128)(2,1)} custom-call(bf16[512,3072]{1,0:T(8,128)(2,1)S(1)} %copy-done, bf16[512,3072]{1,0:T(8,128)(2,1)S(1)} %copy-done, bf16[512,3072]{1,0:T(8,128)(2,1)S(1)} %copy-done, bf16[384,512]{1,0:T(8,128)(2,1)S(1)} %get-tuple-element.12.ck_ref, bf16[384,512]{1,0:T(8,128)(2,1)S(1)} %get-tuple-element.11.cv_ref), custom_call_target="tpu_custom_call" | custom-call | flops 3758096384 | bytes 4194304 | tf_op jit(solution)/shard_map/attend/pallas_call | solution.py:59
  (1 shorter events, 0.0 us)
Async XLA Ops:
  0.9 3.8 %copy-start.1 = (s32[48]{0:T(128)}, s32[48]{0:T(128)S(1)}, u32[]{:S(2)}) copy-start(s32[48]{0:T(128)S(1)} %broadcast_in_dim_reshape.2.owner_ref) | copy-start | bytes 580
  1.1 3.6 %copy-start.2 = (s32[48]{0:T(128)}, s32[48]{0:T(128)S(1)}, u32[]{:S(2)}) copy-start(s32[48]{0:T(128)S(1)} %convert_reduce_fusion.rank_ref) | copy-start | bytes 580
  193.2 2.1 copy-start

commit v5 on v4

--- a/solution.py
+++ b/solution.py
@@ -79,7 +79,7 @@
 
 
 def project_kernel(
-    chips, cores, picks_ref, owner_ref, rank_ref, gain_ref, kv_ref, h_ref, w_ref, o_ref, f_ref,
+    chips, cores, picks_ref, owner_ref, rank_ref, gain_ref, kv_ref, h_ref, wq_ref, wk_ref, wv_ref, o_ref, f_ref,
     held, total, hidden, normed, outbox, inbox, forward, copy_sem, ring_send, ring_recv,
     pair_send, pair_recv, peer_send, peer_recv, spread_send, spread_recv, last_send, last_recv,
 ):
@@ -104,11 +104,17 @@
     left = place_to_chip(lax.rem(spot + chips - 1, chips)) * cores + core
     sibling = chip * cores + (cores - 1 - core)
 
+    half = held.shape[4]
+    rest = wq_ref.shape[1] - half
+    keys = wk_ref.shape[1]
+    later = held.at[1, chip, core]
     own = [
-        pltpu.make_async_copy(w_ref.at[way], held.at[way, chip, core], copy_sem.at[way])
-        for way in range(2)
+        pltpu.make_async_copy(wq_ref.at[:, :half], held.at[0, chip, core], copy_sem.at[0]),
+        pltpu.make_async_copy(wq_ref.at[:, half:], later.at[:, :rest], copy_sem.at[1]),
+        pltpu.make_async_copy(h_ref, hidden.at[mine], copy_sem.at[2]),
+        pltpu.make_async_copy(wk_ref, later.at[:, rest : rest + keys], copy_sem.at[5]),
+        pltpu.make_async_copy(wv_ref, later.at[:, rest + keys :], copy_sem.at[6]),
     ]
-    own.append(pltpu.make_async_copy(h_ref, hidden.at[mine], copy_sem.at[2]))
     for copy in own:
         copy.start()
     barrier = pltpu.get_barrier_semaphore()
@@ -206,7 +212,6 @@
     kept.start()
     total[...] = jnp.zeros_like(total)
 
-    half = held.shape[4]
     depth = cores * held.shape[3]
     width = 256 if half % 256 == 0 else 128
 
@@ -233,7 +238,7 @@
             if cores == 2:
                 pair(way, step, core).start()
 
-    loop(1, length - 1, advance)
+    loop(1, length, advance)
     for k in range(1, peers):
         peer(k, lax.rem(mine + peers - k, peers)).wait_recv()
     rows = hidden.shape[1]
@@ -254,7 +259,7 @@
             normed[source, at, :] = (floats * inverse * gain).astype(jnp.bfloat16)
 
     loop(0, rows // height, normalise)
-    advance(length - 1)
+    advance(length)
     loop(1, devices, lambda k: spread(k, lax.rem(me + devices - k, devices)).wait_recv())
     kept.wait()
 
@@ -272,10 +277,13 @@
         advance(step)
         for early in range(2):
             for way in range(2):
-                compute(way, (step - length) * 2 + early)
-
-    loop(length, chips, second)
+                compute(way, (step - length - 1) * 2 + early)
+
+    loop(length + 1, chips, second)
     for way in range(2):
+        compute(way, chips - 2)
+    for way in range(2):
+        compute(way, chips - 1)
         for begin in range(0, half, width):
             o_ref[:, way * half + begin : way * half + begin + width] = total[
                 way, :, begin : begin + width
@@ -300,17 +308,17 @@
         peer(k, mine).wait_send()
 
 
-def project(hidden_in, norm_gain, stacked, kv_cache, picked, owners, ranks):
+def project(hidden_in, norm_gain, weights, kv_cache, picked, owners, ranks):
     devices = lax.axis_size("context")
     peers = lax.axis_size("tensor")
     cores = 2 if peers == 2 else 1
     chips = devices // cores
     rows, part = hidden_in.shape
-    depth, columns = stacked.shape
+    depth = weights[0].shape[0]
+    columns = sum(weight.shape[1] for weight in weights)
     half = columns // 2
     span = kv_cache.shape[2]
     piece = C_BLOCK // devices
-    split = jnp.stack([stacked[:, :half], stacked[:, half:]])
     smem = pl.BlockSpec(memory_space=pltpu.SMEM)
     vmem = pl.BlockSpec(memory_space=pltpu.VMEM)
     anywhere = pl.BlockSpec(memory_space=pl.ANY)
@@ -321,7 +329,7 @@
             jax.ShapeDtypeStruct((rows, columns), jnp.bfloat16),
             jax.ShapeDtypeStruct((devices, PICKS, piece, 2, span), jnp.bfloat16),
         ),
-        in_specs=[smem, smem, smem, vmem, vmem, anywhere, anywhere],
+        in_specs=[smem, smem, smem, vmem, vmem, anywhere, anywhere, anywhere, anywhere],
         out_specs=(vmem, vmem),
         scratch_shapes=[
             pltpu.VMEM((2, chips, cores, depth, half), jnp.bfloat16),
@@ -331,7 +339,7 @@
             pltpu.VMEM((devices, MOST_REQ, piece, 2, span), jnp.bfloat16),
             pltpu.VMEM((devices, MOST_REQ, piece, 2, span), jnp.bfloat16),
             pltpu.VMEM((devices, PICKS, piece, 2, span), jnp.bfloat16),
-            sems(5),
+            sems(7),
             sems(2, chips),
             sems(2, chips),
             sems(2, chips),
@@ -354,7 +362,7 @@
         norm_gain.reshape(1, -1),
         kv_cache.reshape(BLOCKS_DEV, devices, piece, 2, span),
         hidden_in,
-        split,
+        *weights,
     )
 
 
@@ -362,7 +370,7 @@
     local_heads = kv_cache.shape[2] // HEAD_DIM
     groups = w_query.shape[1] // (HEAD_DIM * local_heads)
     devices = lax.axis_size("context")
-    stacked = jnp.concatenate([w_query, w_key, w_value], axis=1)
+    weights = (w_query, w_key, w_value)
     owners = (selected // BLOCKS_DEV).reshape(devices * PICKS)
     offsets = (selected % BLOCKS_DEV).reshape(devices * PICKS)
     serial = jnp.arange(devices * PICKS, dtype=jnp.int32)
@@ -371,7 +379,7 @@
     slots = jnp.arange(MOST_REQ, dtype=jnp.int32)
     hits = (owners[None, :] == lax.axis_index("context")) & (ranks[None, :] == slots[:, None])
     picked = jnp.sum(jnp.where(hits, offsets[None, :], 0), axis=1)
-    projected, fetched = project(hidden_in, norm_gain, stacked, kv_cache, picked, owners, ranks)
+    projected, fetched = project(hidden_in, norm_gain, weights, kv_cache, picked, owners, ranks)
     fetched = fetched.transpose(1, 0, 2, 3, 4).reshape(PICKS * C_BLOCK, 2, kv_cache.shape[2])
     return attend(projected, fetched[:, 0], fetched[:, 1], groups, local_heads)
 

time: 218 us -> 221 us (1.014)
  Pallas kernels: 206 us -> 213 us
  other arithmetic: 4.27 us -> 1.54 us
    pallas_call x1, Pallas kernels: 187 us -> 195 us  [project(): pl.pallas_call(functools.partial(project_kernel, chips, cores), out_shape...]
    another operation x2 -> x0, other arithmetic: 2.73 us -> none  [project(): split = jnp.stack([stacked[:, :half], stacked[:, half:]])]
where the time goes in v5:
time: 221 us; the launch traced here: 219 us
  Pallas kernels  213 us (96%)
  local copies, waits for them, and re-layouts  3.77 us (2%)
    pallas_call x1, Pallas kernels, project(): pl.pallas_call(functools.partial(project_kernel, chips, cores), out_shape...  195 us
    pallas_call x1, Pallas kernels, attend(): pl.pallas_call(functools.partial(attend_kernel, groups), grid=(local_head...  18.7 us

profile of v5, /device:TPU:13, one launch (start us, length us, event | category | flops | bytes accessed | tf_op | source)
XLA Modules:
  0.0 218.7 jit_solution(9467584691053242188)
XLA Ops:
  0.0 0.7 add_select_fusion.1
  0.7 0.1 copy.14
  0.8 0.1 broadcast_in_dim_reshape.2.owner_ref
  0.9 0.0 copy-start.1
  0.9 0.2 convert_reduce_fusion.rank_ref
  1.1 0.0 copy-start.2
  1.1 0.1 copy.15
  1.2 0.1 broadcast_in_dim.18
  1.2 0.7 select_reduce_fusion.picks_ref
  1.9 1.3 reshape.21.gain_ref
  3.2 0.0 copy-done.1
  3.2 0.0 copy-done.2
  3.2 194.7 %project.1 = (bf16[512,3072]{1,0:T(8,128)(2,1)}, bf16[16,3,8,2,512]{4,3,2,1,0:T(2,128)(2,1)}) custom-call(s32[6]{0:T(128)} %select_reduce_fusion.picks_ref, s32[48]{0:T(128)} %copy-done.1, s32[48]{0:T(128)} %copy-done.2, bf16[1,4096]{1,0:T(2,128)(2,1)} %reshape.21.gain_ref, bf16[8,16,8,2,512]{4,3,2,1,0:T(2,128)(2,1)} %bitcast.8, bf16[512,2048]{1,0:T(8,128)(2,1)} %h_ref.1, ...), custom_call_target="tpu_custom_call" | custom-call | tf_op jit(solution)/shard_map/project/pallas_call | solution.py:326
  197.9 0.0 copy-start
  197.9 1.4 copy.16
  199.3 0.1 slice_bitcast_fusion
  199.3 0.7 copy-done
  200.0 18.7 %attend.1 = bf16[512,2048]{1,0:T(8,128)(2,1)} custom-call(bf16[512,3072]{1,0:T(8,128)(2,1)S(1)} %copy-done, bf16[512,3072]{1,0:T(8,128)(2,1)S(1)} %copy-done, bf16[512,3072]{1,0:T(8,128)(2,1)S(1)} %copy-done, bf16[384,512]{1,0:T(8,128)(2,1)S(1)} %get-tuple-element.10.ck_ref, bf16[384,512]{1,0:T(8,128)(2,1)S(1)} %get-tuple-element.9.cv_ref), custom_call_target="tpu_custom_call" | custom-call | flops 3758096384 | bytes 4194304 | tf_op jit(solution)/shard_map/attend/pallas_call | solution.py:59
  (1 shorter events, 0.0 us)
Async XLA Ops:
  0.9 2.4 %copy-start.1 = (s32[48]{0:T(128)}, s32[48]{0:T(128)S(1)}, u32[]{:S(2)}) copy-start(s32[48]{0:T(128)S(1)} %broadcast_in_dim_reshape.2.owner_ref) | copy-start | bytes 580
  1.1 2.2 copy-start.2
  197.9 2.1 copy-start

commit v6 on v5

--- a/solution.py
+++ b/solution.py
@@ -238,7 +238,7 @@
             if cores == 2:
                 pair(way, step, core).start()
 
-    loop(1, length, advance)
+    loop(1, length - 1, advance)
     for k in range(1, peers):
         peer(k, lax.rem(mine + peers - k, peers)).wait_recv()
     rows = hidden.shape[1]
@@ -259,7 +259,7 @@
             normed[source, at, :] = (floats * inverse * gain).astype(jnp.bfloat16)
 
     loop(0, rows // height, normalise)
-    advance(length)
+    advance(length - 1)
     loop(1, devices, lambda k: spread(k, lax.rem(me + devices - k, devices)).wait_recv())
     kept.wait()
 
@@ -277,13 +277,10 @@
         advance(step)
         for early in range(2):
             for way in range(2):
-                compute(way, (step - length - 1) * 2 + early)
-
-    loop(length + 1, chips, second)
+                compute(way, (step - length) * 2 + early)
+
+    loop(length, chips, second)
     for way in range(2):
-        compute(way, chips - 2)
-    for way in range(2):
-        compute(way, chips - 1)
         for begin in range(0, half, width):
             o_ref[:, way * half + begin : way * half + begin + width] = total[
                 way, :, begin : begin + width

time: 221 us -> 215 us (0.973)
  Pallas kernels: 213 us -> 206 us
    pallas_call x1, Pallas kernels: 195 us -> 187 us  [project(): pl.pallas_call(functools.partial(project_kernel, chips, cores), out_shape...]
where the time goes in v6:
time: 215 us; the launch traced here: 211 us
  Pallas kernels  206 us (96%)
  local copies, waits for them, and re-layouts  3.77 us (2%)
    pallas_call x1, Pallas kernels, project(): pl.pallas_call(functools.partial(project_kernel, chips, cores), out_shape...  187 us
    pallas_call x1, Pallas kernels, attend(): pl.pallas_call(functools.partial(attend_kernel, groups), grid=(local_head...  18.6 us

profile of v6, /device:TPU:13, one launch (start us, length us, event | category | flops | bytes accessed | tf_op | source)
XLA Modules:
  0.0 211.3 jit_solution(8448942404568664530)
XLA Ops:
  0.0 0.7 add_select_fusion.1
  0.7 0.1 copy.14
  0.8 0.1 broadcast_in_dim_reshape.2.owner_ref
  0.9 0.0 copy-start.1
  0.9 0.2 convert_reduce_fusion.rank_ref
  1.1 0.0 copy-start.2
  1.1 0.1 copy.15
  1.2 0.1 broadcast_in_dim.18
  1.2 0.7 select_reduce_fusion.picks_ref
  1.9 1.3 reshape.21.gain_ref
  3.2 0.0 copy-done.1
  3.2 0.0 copy-done.2
  3.2 187.3 %project.1 = (bf16[512,3072]{1,0:T(8,128)(2,1)}, bf16[16,3,8,2,512]{4,3,2,1,0:T(2,128)(2,1)}) custom-call(s32[6]{0:T(128)} %select_reduce_fusion.picks_ref, s32[48]{0:T(128)} %copy-done.1, s32[48]{0:T(128)} %copy-done.2, bf16[1,4096]{1,0:T(2,128)(2,1)} %reshape.21.gain_ref, bf16[8,16,8,2,512]{4,3,2,1,0:T(2,128)(2,1)} %bitcast.8, bf16[512,2048]{1,0:T(8,128)(2,1)} %h_ref.1, ...), custom_call_target="tpu_custom_call" | custom-call | tf_op jit(solution)/shard_map/project/pallas_call | solution.py:323
  190.6 0.0 copy-start
  190.6 1.4 copy.16
  191.9 0.1 slice_bitcast_fusion
  192.0 0.7 copy-done
  192.7 18.6 %attend.1 = bf16[512,2048]{1,0:T(8,128)(2,1)} custom-call(bf16[512,3072]{1,0:T(8,128)(2,1)S(1)} %copy-done, bf16[512,3072]{1,0:T(8,128)(2,1)S(1)} %copy-done, bf16[512,3072]{1,0:T(8,128)(2,1)S(1)} %copy-done, bf16[384,512]{1,0:T(8,128)(2,1)S(1)} %get-tuple-element.10.ck_ref, bf16[384,512]{1,0:T(8,128)(2,1)S(1)} %get-tuple-element.9.cv_ref), custom_call_target="tpu_custom_call" | custom-call | flops 3758096384 | bytes 4194304 | tf_op jit(solution)/shard_map/attend/pallas_call | solution.py:59
  (1 shorter events, 0.0 us)
Async XLA Ops:
  0.9 2.4 %copy-start.1 = (s32[48]{0:T(128)}, s32[48]{0:T(128)S(1)}, u32[]{:S(2)}) copy-start(s32[48]{0:T(128)S(1)} %broadcast_in_dim_reshape.2.owner_ref) | copy-start | bytes 580
  1.1 2.2 %copy-start.2 = (s32[48]{0:T(128)}, s32[48]{0:T(128)S(1)}, u32[]{:S(2)}) copy-start(s32[48]{0:T(128)S(1)} %convert_reduce_fusion.rank_ref) | copy-start | bytes 580
  190.6 2.1 %copy-start = (bf16[512,3072]{1,0:T(8,128)(2,1)S(1)}, bf16[512,3072]{1,0:T(8,128)(2,1)}, u32[]{:S(2)}) copy-start(bf16[512,3072]{1,0:T(8,128)(2,1)} %get-tuple-element.7.q_ref.k_ref.v_ref) | copy-start | bytes 9437188
